TPU v7x, 256 devices: a whole 4x4x8 slice. The times are simulated.
256 devices in a mesh: blocks: 64 (over x, z, core), rep: 4 (over y).
Axes of the slice: x: 4, y: 4, z: 8, core: 2. Of those that a mesh axis runs over, the one named last changes fastest.
Arguments:
- features: bfloat16 [4, 256, 512, 128], P('rep', 'blocks'), may hold values from -6 to 6
- weight_one: bfloat16 [27, 128, 128], replicated, may hold values from -0.109375 to 0.109375
- weight_two: bfloat16 [27, 128, 128], replicated, may hold values from -0.109375 to 0.109375
- cotangent: bfloat16 [4, 256, 512, 128], P('rep', 'blocks'), may hold values from -6 to 6
- neighbours: int32 [4, 256, 26], P('rep', 'blocks'), may hold values from -1 to 255, as said below
Outputs:
- segment_out: bfloat16 [4, 256, 512, 128], P('rep', 'blocks')
- grad_one: float32 [27, 128, 128], replicated
- grad_two: float32 [27, 128, 128], replicated
Inputs may be any that keep to these rules, and one draw needn't show every extreme that they name: neighbours[s, b, k] is the active block at offset k from block b in the slab of scene s, or -1 where that block is empty or outside the slab; blocks are ordered by x, then within each cross-section of 4 x 4 blocks by the Morton alternate of y and z, taken in reverse on odd x; block b belongs to device b // 4 of the axis blocks; the relation is symmetric (b names n at an offset exactly when n names b at the opposite one); the devices of a block and of any of its neighbours differ by at most 7 in index, and in every scene some pair differs by exactly 7.
All inputs are finite; a program needn't handle non-finite values.
Results may differ from a plain program's by a relative error of at most 0.005.
Values may be sent and summed in bfloat16 or wider, within the bound.
No kernel may reach another device: no remote copies, remote signals or barrier semaphores. Data moves between devices by JAX's collectives and lax.ppermute only.
A program may use at most 128 MiB of HBM per device.

v0:
```python
import math

import jax
import jax.numpy as jnp
from jax import lax
from jax.experimental import pallas as pl
from jax.experimental.pallas import tpu as pltpu
from jax.sharding import PartitionSpec as P


CH = 128
BD = 4
RX, RE, RP = 256, 128, 256
FULL, MID, FAR = RX + RE + 2 * RP, RX + RE, RX
SLOTS = 20

OFFSETS = [
    (dx, dy, dz)
    for dx in (-1, 0, 1)
    for dy in (-1, 0, 1)
    for dz in (-1, 0, 1)
    if (dx, dy, dz) != (0, 0, 0)
]
K_OF = {offset: k for k, offset in enumerate(OFFSETS)}
BF = jnp.bfloat16
F32 = jnp.float32


def pack_field(nb, dev, own, down, up, fields, f):
    ox, oe = f * RX, fields * RX + f * RE
    oj = fields * (RX + RE) + f * RP
    ol = fields * (RX + RE + RP) + f * RP

    def body(b, carry):
        me = dev * BD + b

        def neighbour(offset):
            return nb[b, K_OF[offset]]

        y_hi, y_lo = neighbour((0, 1, 0)), neighbour((0, -1, 0))
        z_hi, z_lo = neighbour((0, 0, 1)), neighbour((0, 0, -1))
        cases = (
            (down, 0, (y_hi >= 0) & (y_hi < me), (z_hi >= 0) & (z_hi < me)),
            (up, 448, jnp.logical_not(y_lo > me), jnp.logical_not(z_lo > me)),
        )
        edges = jnp.concatenate(
            [own[b, pl.ds(js * 8 + ls, 8, stride=64), :] for js in (0, 7) for ls in (0, 7)], axis=0
        ).astype(BF)
        z_low = own[b, pl.ds(0, 64, stride=8), :]
        z_high = own[b, pl.ds(7, 64, stride=8), :]
        y_low = jnp.concatenate([own[b, i * 64 : i * 64 + 8, :] for i in range(8)], axis=0)
        y_high = jnp.concatenate([own[b, i * 64 + 56 : i * 64 + 64, :] for i in range(8)], axis=0)
        for ref, x_row, take_y, take_z in cases:
            ref[pl.ds(pl.multiple_of(ox + b * 64, 64), 64), :] = own[b, x_row : x_row + 64, :].astype(BF)
            ref[pl.ds(pl.multiple_of(oe + b * 32, 32), 32), :] = edges
            ref[pl.ds(pl.multiple_of(oj + b * 64, 64), 64), :] = jnp.where(take_y, y_high, y_low).astype(BF)
            ref[pl.ds(pl.multiple_of(ol + b * 64, 64), 64), :] = jnp.where(take_z, z_high, z_low).astype(BF)
        return carry

    lax.fori_loop(0, BD, body, 0)


def fill_tables(core, pieces, tx, te, tj, tl, fields, f):
    own_down, own_up, d1, u1, d2, u2, d3, u3, v4, near, wide = pieces
    full, mid, far = fields * FULL, fields * MID, fields * FAR
    turn = 2 * core
    plan = [
        (own_down, 0, 10, 4),
        (own_up, 0, 9, 4),
        (d1, 0, 12, 4),
        (u1, 0, 7, 4),
        (d2, 0, 14, 2),
        (u2, 0, 5, 2),
        (d3, 0, 16, 1),
        (u3, 0, 3, 1),
        (v4, 0, 2 + 15 * core, 1),
        (near, 0, 11 - 3 * core, 4),
        (near, full, 13 - turn, 4),
        (near, 2 * full, 8 - turn, 4),
        (wide, 0, 15 - turn, 2),
        (wide, mid, 6 - turn, 2),
        (wide, 2 * mid, 17 - turn, 1),
        (wide, 2 * mid + far, 4 - turn, 1),
    ]
    for ref, base, slot, kind in plan:
        row = base + f * RX
        tx[slot] = ref[row : row + RX, :].astype(F32).reshape(BD, 64, CH)
        if kind >= 2:
            row = base + fields * RX + f * RE
            te[slot] = ref[row : row + RE, :].astype(F32).reshape(BD, 32, CH)
        if kind >= 4:
            row = base + fields * (RX + RE) + f * RP
            tj[slot] = ref[row : row + RP, :].astype(F32).reshape(BD, 64, CH)
            row += fields * RP
            tl[slot] = ref[row : row + RP, :].astype(F32).reshape(BD, 64, CH)


def build_shifted(nb, dev, own, tx, te, tj, tl, cf, lf, rf, sh):
    def block(b, carry):
        me = dev * BD + b

        def source(offset):
            n = nb[b, K_OF[offset]]
            gap = lax.shift_right_logical(jnp.maximum(n, 0), 2) - dev
            slot = jnp.clip(jnp.where(n > me, 10 + gap, 9 + gap), 0, SLOTS - 1)
            return n >= 0, slot, jnp.maximum(n, 0) & 3

        def keep(valid, rows):
            return jnp.where(valid, rows, jnp.zeros_like(rows))

        for i in range(8):
            cf[b, pl.ds((i + 1) * 80 + 8, 64), :] = own[b, pl.ds(i * 64, 64), :]
        for dy, line in ((-1, 0), (1, 9)):
            valid, slot, loc = source((0, dy, 0))
            for i in range(8):
                rows = tj[slot, loc, pl.ds(i * 8, 8), :]
                cf[b, pl.ds((i + 1) * 80 + line * 8, 8), :] = keep(valid, rows)
        for dx, plane in ((-1, 0), (1, 9)):
            valid, slot, loc = source((dx, 0, 0))
            cf[b, pl.ds(plane * 80 + 8, 64), :] = keep(valid, tx[slot, loc])
            for dy, line, j in ((-1, 0, 7), (1, 9, 0)):
                valid, slot, loc = source((dx, dy, 0))
                rows = tx[slot, loc, pl.ds(j * 8, 8), :]
                cf[b, pl.ds(plane * 80 + line * 8, 8), :] = keep(valid, rows)
        for plane in range(10):
            lines = cf[b, pl.ds(plane * 80, 80), :].reshape(10, 8, CH)
            lf[b, pl.ds(plane * 80, 80), :] = pltpu.roll(lines, 1, 1).reshape(80, CH)
            rf[b, pl.ds(plane * 80, 80), :] = pltpu.roll(lines, 7, 1).reshape(80, CH)
        for dz, ref, cell, l in ((-1, lf, 0, 7), (1, rf, 7, 0)):
            valid, slot, loc = source((0, 0, dz))
            for i in range(8):
                rows = tl[slot, loc, pl.ds(i * 8, 8), :]
                ref[b, pl.ds((i + 1) * 80 + 8 + cell, 8, stride=8), :] = keep(valid, rows)
            for dy, line, j in ((-1, 0, 7), (1, 9, 0)):
                valid, slot, loc = source((0, dy, dz))
                edge = (2 * (j // 7) + l // 7) * 8
                rows = te[slot, loc, pl.ds(edge, 8), :]
                ref[b, pl.ds(80 + line * 8 + cell, 8, stride=80), :] = keep(valid, rows)
            for dx, plane in ((-1, 0), (1, 9)):
                valid, slot, loc = source((dx, 0, dz))
                rows = tx[slot, loc, pl.ds(l, 8, stride=8), :]
                ref[b, pl.ds(plane * 80 + 8 + cell, 8, stride=8), :] = keep(valid, rows)
                for dy, line, j in ((-1, 0, 7), (1, 9, 0)):
                    valid, slot, loc = source((dx, dy, dz))
                    rows = tx[slot, loc, pl.ds(j * 8 + l, 1), :]
                    ref[b, pl.ds(plane * 80 + line * 8 + cell, 1), :] = keep(valid, rows)
        return carry

    lax.fori_loop(0, BD, block, 0)

    def join(plane, carry):
        row = pl.multiple_of(plane * 80, 80)
        for pair in range(2):
            for c, ref in ((0, lf), (1, cf), (2, rf)):
                halves = [ref[2 * pair + h, pl.ds(row, 80), :].reshape(10, 8, CH) for h in (0, 1)]
                sh[c, pair, plane] = jnp.concatenate(halves, axis=1).astype(BF)
        return carry

    lax.fori_loop(0, 10, join, 0)


def slabs(sh, pair, first, count, taps):
    return jnp.concatenate(
        [
            sh[c, pair, pl.ds(first + a, count), b : b + 8].reshape(count * 128, CH)
            for a, b, c in taps
        ],
        axis=1,
    )


TAPS = [(a, b, c) for a in range(3) for b in range(3) for c in range(3)]
CHUNK = 4


def conv(sh, weight, emit):
    def body(step, carry):
        pair = step // (8 // CHUNK)
        first = (step % (8 // CHUNK)) * CHUNK
        rows = jnp.dot(slabs(sh, pair, first, CHUNK, TAPS), weight[...], preferred_element_type=F32)
        emit(pair, first, rows)
        return carry

    lax.fori_loop(0, 2 * (8 // CHUNK), body, 0)


def split_blocks(pair, first, rows, store):
    lines = rows.reshape(CHUNK * 8, 16, CH)
    for h in (0, 1):
        part = lines[:, 8 * h : 8 * h + 8].reshape(CHUNK * 64, CH)
        store(2 * pair + h, pl.multiple_of(first * 64, 64), part)


def load_own(ref, own):
    for b in range(BD):
        own[b] = ref[b].astype(F32)


def pack_kernel(nb, dev, feat, cot, down, up, own):
    for f, ref in enumerate((feat, cot)):
        load_own(ref, own)
        pack_field(nb, dev[0], own, down, up, 2, f)


def forward_kernel(nb, dev, feat, *refs):
    pieces, weight = refs[:11], refs[11]
    hid, hid_s, pre, down, up, sh, own, tx, te, tj, tl, cf, lf, rf = refs[12:]
    load_own(feat, own)
    fill_tables(dev[0] & 1, pieces, tx, te, tj, tl, 2, 0)
    build_shifted(nb, dev[0], own, tx, te, tj, tl, cf, lf, rf, sh)

    def emit(pair, first, rows):
        at = pl.ds(pl.multiple_of(pair * 1024 + first * 128, 128), CHUNK * 128)
        pre[at, :] = rows
        act = (rows / (1.0 + jnp.exp(-rows))).astype(BF)
        hid_s[at, :] = act

        def store(b, row, part):
            own[b, pl.ds(row, CHUNK * 64), :] = part
            hid[b, pl.ds(row, CHUNK * 64), :] = part.astype(BF)

        split_blocks(pair, first, act.astype(F32), store)

    conv(sh, weight, emit)
    pack_field(nb, dev[0], own, down, up, 1, 0)


def backward_kernel(nb, dev, cot, *refs):
    pieces, weight, hid_s, pre = refs[:11], refs[11], refs[12], refs[13]
    sh, hid_t, delta_t, own, tx, te, tj, tl, cf, lf, rf, delta = refs[14:]
    load_own(cot, own)
    fill_tables(dev[0] & 1, pieces, tx, te, tj, tl, 2, 1)
    build_shifted(nb, dev[0], own, tx, te, tj, tl, cf, lf, rf, sh)

    def emit(pair, first, rows):
        at = pl.ds(pl.multiple_of(pair * 1024 + first * 128, 128), CHUNK * 128)
        v = pre[at, :]
        sig = 1.0 / (1.0 + jnp.exp(-v))
        delta[at, :] = (rows * (sig * (1.0 + v * (1.0 - sig)))).astype(BF)

    conv(sh, weight, emit)
    for pair in range(2):
        hid_t[pair] = hid_s[pair * 1024 : pair * 1024 + 1024, :].T
        delta_t[pair] = delta[pair * 1024 : pair * 1024 + 1024, :].T


def gradient_kernel(nb, dev, hid_t, delta_t, sh_feat, sh, keep, send):
    def body(step, carry):
        a, b = step // 3, step % 3

        def product(left, ref):
            total = None
            for pair in range(2):
                right = jnp.concatenate(
                    [ref[c, pair, pl.ds(a, 8), pl.ds(b, 8)].reshape(1024, CH) for c in range(3)], axis=1
                )
                term = jnp.dot(left[pair], right, preferred_element_type=F32)
                total = term if total is None else total + term
            return total

        one = product(delta_t, sh_feat)
        two = product(hid_t, sh)

        def write(first, second):
            for c in range(3):
                row = pl.multiple_of((step * 3 + c) * CH, CH)
                first[pl.ds(row, CH), :] = one[:, c * CH : c * CH + CH].T
                row = pl.multiple_of((26 - step * 3 - c) * CH, CH)
                second[pl.ds(row, CH), :] = two[:, c * CH : c * CH + CH]

        @pl.when((dev[0] & 1) == 0)
        def _():
            write(keep, send)

        @pl.when((dev[0] & 1) == 1)
        def _():
            write(send, keep)

        return carry

    lax.fori_loop(0, 9, body, 0)


def second_kernel(nb, dev, hid, *refs):
    pieces, weight, out = refs[:11], refs[11], refs[12]
    own, tx, te, tj, tl, cf, lf, rf, sh = refs[13:]
    load_own(hid, own)
    fill_tables(dev[0] & 1, pieces, tx, te, tj, tl, 1, 0)
    build_shifted(nb, dev[0], own, tx, te, tj, tl, cf, lf, rf, sh)

    def emit(pair, first, rows):
        def store(b, row, part):
            out[b, pl.ds(row, CHUNK * 64), :] = part.astype(BF)

        split_blocks(pair, first, rows, store)

    conv(sh, weight, emit)


def scratch_own():
    return [pltpu.VMEM((BD, 512, CH), F32)]


def scratch_build():
    return [
        pltpu.VMEM((SLOTS, BD, 64, CH), F32),
        pltpu.VMEM((SLOTS, BD, 32, CH), F32),
        pltpu.VMEM((SLOTS, BD, 64, CH), F32),
        pltpu.VMEM((SLOTS, BD, 64, CH), F32),
    ] + [pltpu.VMEM((BD, 800, CH), F32)] * 3


SHIFTED = (3, 2, 10, 10, 16, CH)


def call(kernel, outs, scratch, nb, dev, *arrays):
    smem = pl.BlockSpec(memory_space=pltpu.SMEM)
    vmem = pl.BlockSpec(memory_space=pltpu.VMEM)
    return pl.pallas_call(
        kernel,
        out_shape=[jax.ShapeDtypeStruct(shape, dtype) for shape, dtype in outs],
        in_specs=[smem, smem] + [vmem] * len(arrays),
        out_specs=[vmem] * len(outs),
        scratch_shapes=scratch,
    )(nb, dev, *arrays)


def hop(x, shift):
    size = lax.axis_size("blocks")
    return lax.ppermute(x, "blocks", [(i, (i + shift(i)) % size) for i in range(size)])


def swap(x):
    return hop(x, lambda i: 1 - 2 * (i % 2))


def exchange_near(down, up):
    return hop(down, lambda i: -2), hop(up, lambda i: 2)


def exchange_rest(down, up, d1, u1, fields, core):
    mid, far = fields * MID, fields * FAR
    last = jnp.where(core == 0, d1[:far], u1[:far])
    v4 = hop(last, lambda i: -5 if i % 2 == 0 else 5)
    d3, u3 = hop(d1[:far], lambda i: -4), hop(u1[:far], lambda i: 4)
    d2, u2 = hop(d1[:mid], lambda i: -2), hop(u1[:mid], lambda i: 2)
    mine = jnp.where(core == 0, up, down)
    near = swap(jnp.concatenate([mine, d1, u1], axis=0))
    wide = swap(jnp.concatenate([d2, u2, d3, u3], axis=0))
    return (down, up, d1, u1, d2, u2, d3, u3, v4, near, wide)


def all_to_all(x, axes, groups):
    return lax.all_to_all(x, axes, 0, 0, axis_index_groups=groups, tiled=True)


def reduce_all(keep, send, core, scale, work, given):
    size, reps = lax.axis_size("blocks"), lax.axis_size("rep")
    length = 8
    width = size // (2 * length)
    planes = [
        [(2 * length * x + 2 * z + c) * reps + r for x in range(width) for r in range(reps)]
        for z in range(length)
        for c in range(2)
    ]
    columns = [
        [2 * length * x + 2 * z + c for z in range(length)] for x in range(width) for c in range(2)
    ]
    both = ("blocks", "rep")
    count = width * reps
    rows = keep.shape[0] // count
    mine = keep + swap(send)
    part = all_to_all(mine.astype(BF).reshape(count, rows, CH), both, planes)
    part = jnp.sum(part.astype(F32), axis=0).astype(BF)
    part, given = lax.optimization_barrier((part, given))
    done = work(given)
    part = jnp.broadcast_to(part[None], (length, rows, CH))
    part = all_to_all(part, "blocks", columns)
    part = (jnp.sum(part.astype(F32), axis=0) * scale).astype(BF)
    part, done = lax.optimization_barrier((part, done))
    part = jnp.broadcast_to(part[None], (count, rows, CH))
    mine = all_to_all(part, both, planes).reshape(keep.shape)
    theirs = swap(mine)
    shape = (keep.shape[0] // CH, CH, CH)
    one = jnp.where(core == 0, mine, theirs).astype(F32).reshape(shape)
    two = jnp.where(core == 0, theirs, mine).astype(F32).reshape(shape)
    return one, two, done


def slab_step(features, weight_one, weight_two, cotangent, neighbours):
    feat, cot, nb = features[0], cotangent[0], neighbours[0]
    index = lax.axis_index("blocks")
    core = index % 2
    dev = index.astype(jnp.int32).reshape(1)
    w_one = weight_one.reshape(27 * CH, CH)
    w_two = weight_two.reshape(27 * CH, CH)
    flipped = jnp.transpose(weight_two[::-1], (0, 2, 1)).reshape(27 * CH, CH)
    two_fields = (2 * FULL, CH)
    down, up = call(pack_kernel, [(two_fields, BF)] * 2, scratch_own(), nb, dev, feat, cot)
    d1, u1 = exchange_near(down, up)
    pieces = exchange_rest(down, up, d1, u1, 2, core)
    hid, hid_s, pre, hid_down, hid_up, sh_feat = call(
        forward_kernel,
        [
            ((BD, 512, CH), BF),
            ((BD * 512, CH), BF),
            ((BD * 512, CH), F32),
            ((FULL, CH), BF),
            ((FULL, CH), BF),
            (SHIFTED, BF),
        ],
        scratch_own() + scratch_build(),
        nb,
        dev,
        feat,
        *pieces,
        w_one,
    )
    d1, u1 = exchange_near(hid_down, hid_up)
    sh_cot, hid_t, delta_t = call(
        backward_kernel,
        [(SHIFTED, BF), ((2, CH, 1024), BF), ((2, CH, 1024), BF)],
        scratch_own() + scratch_build() + [pltpu.VMEM((BD * 512, CH), BF)],
        nb,
        dev,
        cot,
        *pieces,
        flipped,
        hid_s,
        pre,
    )
    d1, u1, hid_t, delta_t, sh_cot = lax.optimization_barrier((d1, u1, hid_t, delta_t, sh_cot))
    hid_pieces = exchange_rest(hid_down, hid_up, d1, u1, 1, core)
    keep, send = call(
        gradient_kernel,
        [((27 * CH, CH), F32)] * 2,
        [],
        nb,
        dev,
        hid_t,
        delta_t,
        sh_feat,
        sh_cot,
    )
    (keep, send), hid_pieces = lax.optimization_barrier(((keep, send), hid_pieces))
    voxel_total = lax.axis_size("rep") * lax.axis_size("blocks") * BD * 512
    scale = 1.0 / math.sqrt(voxel_total)

    def second(hid):
        return call(
            second_kernel,
            [((BD, 512, CH), BF)],
            scratch_own() + scratch_build() + [pltpu.VMEM(SHIFTED, BF)],
            nb,
            dev,
            hid,
            *hid_pieces,
            w_two,
        )[0]

    grad_one, grad_two, out = reduce_all(keep, send, core, scale, second, hid)
    return out[None], grad_one, grad_two


def solution(mesh):
    in_specs = (
        P("rep", "blocks", None, None),
        P(),
        P(),
        P("rep", "blocks", None, None),
        P("rep", "blocks", None),
    )
    out_specs = (P("rep", "blocks", None, None), P(), P())
    return jax.shard_map(slab_step, mesh=mesh, in_specs=in_specs, out_specs=out_specs, check_vma=False)
```

profile of v0, /device:TPU:1, one launch (start us, length us, event | category | flops | bytes accessed | tf_op | source)
XLA Modules:
  0.0 183.5 jit_solution(16579706425167003963)
XLA Ops:
  0.6 2.7 %shard_map.76 = (bf16[1792,128]{1,0:T(8,128)(2,1)}, bf16[1792,128]{1,0:T(8,128)(2,1)}) custom-call(s32[4,26]{1,0:T(4,128)} %bitcast.30, s32[1]{0:T(128)} %bitcast.1.dev, bf16[4,512,128]{2,1,0:T(8,128)(2,1)} %bitcast.24, bf16[4,512,128]{2,1,0:T(8,128)(2,1)} %bitcast.26), custom_call_target="tpu_custom_call" | custom-call | tf_op jit(solution)/shard_map/pallas_call | solution.py:319
  3.3 8.6 %collective-permute-start = (bf16[1792,128]{1,0:T(8,128)(2,1)}, bf16[1792,128]{1,0:T(8,128)(2,1)S(1)}, u32[]{:S(2)}, u32[]{:S(2)}) collective-permute-start(bf16[1792,128]{1,0:T(8,128)(2,1)} %get-tuple-element.38.refs_0_), channel_id=1, source_target_pairs={{0,248},{4,252},{8,0},{12,4},{16,8},{20,12},{24,16},{28,20},{32,24... | collective-permute-start | bytes 1376264 | tf_op jit(solution)/shard_map/ppermute | solution.py:330
  13.0 8.4 %collective-permute-done.refs_2_ = bf16[1792,128]{1,0:T(8,128)(2,1)S(1)} collective-permute-done((bf16[1792,128]{1,0:T(8,128)(2,1)}, bf16[1792,128]{1,0:T(8,128)(2,1)S(1)}, u32[]{:S(2)}, u32[]{:S(2)}) %collective-permute-start) | collective-permute-done | bytes 458784 | tf_op jit(solution)/shard_map/ppermute | solution.py:330
  21.4 5.5 %collective-permute-start.2 = (bf16[768,128]{1,0:T(8,128)(2,1)S(1)}, bf16[768,128]{1,0:T(8,128)(2,1)S(1)}, u32[]{:S(2)}, u32[]{:S(2)}) collective-permute-start(bf16[768,128]{1,0:T(8,128)(2,1)S(1)} %slice.36), channel_id=1, source_target_pairs={{0,248},{4,252},{8,0},{12,4},{16,8},{20,12},{24,16},{28,20},{32,24... | collective-permute-start | bytes 589832 | tf_op jit(solution)/shard_map/ppermute | solution.py:330
  33.1 5.5 %collective-permute-done.4.refs_6_ = bf16[512,128]{1,0:T(8,128)(2,1)S(1)} collective-permute-done((bf16[512,128]{1,0:T(8,128)(2,1)S(1)}, bf16[512,128]{1,0:T(8,128)(2,1)S(1)}, u32[]{:S(2)}, u32[]{:S(2)}) %collective-permute-start.4) | collective-permute-done | bytes 131104 | tf_op jit(solution)/shard_map/ppermute | solution.py:330
  38.6 5.5 %collective-permute-done.5.refs_7_ = bf16[512,128]{1,0:T(8,128)(2,1)S(1)} collective-permute-done((bf16[512,128]{1,0:T(8,128)(2,1)S(1)}, bf16[512,128]{1,0:T(8,128)(2,1)S(1)}, u32[]{:S(2)}, u32[]{:S(2)}) %collective-permute-start.5) | collective-permute-done | bytes 131104 | tf_op jit(solution)/shard_map/ppermute | solution.py:330
  47.7 4.9 %collective-permute-done.6.refs_8_ = bf16[512,128]{1,0:T(8,128)(2,1)} collective-permute-done((bf16[512,128]{1,0:T(8,128)(2,1)}, bf16[512,128]{1,0:T(8,128)(2,1)}, u32[]{:S(2)}, u32[]{:S(2)}) %collective-permute-start.6) | collective-permute-done | bytes 131104 | tf_op jit(solution)/shard_map/ppermute | solution.py:330
  53.7 11.2 %shard_map.77 = (bf16[4,512,128]{2,1,0:T(8,128)(2,1)}, bf16[2048,128]{1,0:T(8,128)(2,1)}, f32[2048,128]{1,0:T(8,128)}, bf16[896,128]{1,0:T(8,128)(2,1)}, bf16[89...) custom-call(s32[4,26]{1,0:T(4,128)} %bitcast.31, s32[1]{0:T(128)} %bitcast.1.dev, ...), custom_call_target="tpu_custom_call" | custom-call | tf_op jit(solution)/shard_map/pallas_call | solution.py:319
  64.9 5.8 %collective-permute-start.9 = (bf16[896,128]{1,0:T(8,128)(2,1)}, bf16[896,128]{1,0:T(8,128)(2,1)S(1)}, u32[]{:S(2)}, u32[]{:S(2)}) collective-permute-start(bf16[896,128]{1,0:T(8,128)(2,1)} %get-tuple-element.60.refs_0_), channel_id=1, source_target_pairs={{0,248},{4,252},{8,0},{12,4},{16,8},{20,12},{24,16},{28,20},{32,24... | collective-permute-start | bytes 688136 | tf_op jit(solution)/shard_map/ppermute | solution.py:330
  70.7 10.5 %shard_map.78 = (bf16[3,2,10,10,16,128]{5,4,3,2,1,0:T(8,128)(2,1)}, bf16[2,128,1024]{2,1,0:T(8,128)(2,1)}, bf16[2,128,1024]{2,1,0:T(8,128)(2,1)}) custom-call(s32[4,26]{1,0:T(4,128)} %bitcast.32, s32[1]{0:T(128)} %bitcast.1.dev, bf16[4,512,128]{2,1,0:T(8,128)(2,1)} %bitcast.27, bf16[1792,128]{1,0:T(8,128)(2,1)} %get-tuple-element.38.refs_0_, ...), custom_call_target="tpu_custom_call" | custom-call | tf_op jit(solution)/shard_map/pallas_call | solution.py:319
  82.2 4.2 %collective-permute-start.11 = (bf16[384,128]{1,0:T(8,128)(2,1)S(1)}, bf16[384,128]{1,0:T(8,128)(2,1)S(1)}, u32[]{:S(2)}, u32[]{:S(2)}) collective-permute-start(bf16[384,128]{1,0:T(8,128)(2,1)S(1)} %slice.32), channel_id=1, source_target_pairs={{0,248},{4,252},{8,0},{12,4},{16,8},{20,12},{24,16},{28,20},{32,24... | collective-permute-start | bytes 294920 | tf_op jit(solution)/shard_map/ppermute | solution.py:330
  86.5 2.2 %collective-permute-start.16 = (bf16[2688,128]{1,0:T(8,128)(2,1)S(1)}, bf16[2688,128]{1,0:T(8,128)(2,1)S(1)}, u32[]{:S(2)}, u32[]{:S(2)}) collective-permute-start(bf16[2688,128]{1,0:T(8,128)(2,1)S(1)} %pad_maximum_fusion.1), channel_id=1, source_target_pairs={{0,4},{4,0},{8,12},{12,8},{16,20},{20,16},{24,28},{28,24},{32,36},... | collective-permute-start | bytes 2064392 | tf_op jit(solution)/shard_map/ppermute | solution.py:330
  88.8 2.4 %collective-permute-start.14 = (bf16[256,128]{1,0:T(8,128)(2,1)S(1)}, bf16[256,128]{1,0:T(8,128)(2,1)S(1)}, u32[]{:S(2)}, u32[]{:S(2)}) collective-permute-start(bf16[256,128]{1,0:T(8,128)(2,1)S(1)} %get-tuple-element.80), channel_id=1, source_target_pairs={{0,16},{4,20},{8,24},{12,28},{16,32},{20,36},{24,40},{28,44},{32,4... | collective-permute-start | bytes 196616 | tf_op jit(solution)/shard_map/ppermute | solution.py:330
  91.2 2.2 %collective-permute-done.13.refs_6_ = bf16[256,128]{1,0:T(8,128)(2,1)S(1)} collective-permute-done((bf16[256,128]{1,0:T(8,128)(2,1)S(1)}, bf16[256,128]{1,0:T(8,128)(2,1)S(1)}, u32[]{:S(2)}, u32[]{:S(2)}) %collective-permute-start.13) | collective-permute-done | bytes 65568 | tf_op jit(solution)/shard_map/ppermute | solution.py:330
  93.3 3.4 %collective-permute-done.14.refs_7_ = bf16[256,128]{1,0:T(8,128)(2,1)S(1)} collective-permute-done((bf16[256,128]{1,0:T(8,128)(2,1)S(1)}, bf16[256,128]{1,0:T(8,128)(2,1)S(1)}, u32[]{:S(2)}, u32[]{:S(2)}) %collective-permute-start.14) | collective-permute-done | bytes 65568 | tf_op jit(solution)/shard_map/ppermute | solution.py:330
  97.9 12.2 %shard_map.79 = (f32[3456,128]{1,0:T(8,128)}, f32[3456,128]{1,0:T(8,128)}) custom-call(s32[4,26]{1,0:T(4,128)} %bitcast.33, s32[1]{0:T(128)} %bitcast.1.dev, bf16[2,128,1024]{2,1,0:T(8,128)(2,1)} %get-tuple-element.47.hid_t, bf16[2,128,1024]{2,1,0:T(8,128)(2,1)} %get-tuple-element.48.delta_t, bf16[3,2,10,10,16,128]{5,4,3,2,1,0:T(8,128)(2,1)} %get-tuple-element.49.sh_feat, ...), custom_call_target="tpu_custom_call" | custom-call | tf_op jit(solution)/shard_map/pallas_call | solution.py:319
  110.3 3.9 %collective-permute-done.18 = f32[3456,128]{1,0:T(8,128)S(1)} collective-permute-done((f32[3456,128]{1,0:T(8,128)}, f32[3456,128]{1,0:T(8,128)S(1)}, u32[]{:S(2)}, u32[]{:S(2)}) %collective-permute-start.18) | collective-permute-done | bytes 1769504 | tf_op jit(solution)/shard_map/ppermute | solution.py:330
  115.9 18.2 %all_to_all.15 = bf16[16,216,128]{2,1,0:T(8,128)(2,1)S(1)} all-to-all(bf16[16,216,128]{2,1,0:T(8,128)(2,1)S(1)} %bitcast.23), channel_id=1, replica_groups={{0,1,2,3,64,65,66,67,128,129,130,131,192,193,194,195},{4,5,6,7,68,69,70..., dimensions={0} | all-to-all | bytes 1769472 | tf_op jit(solution)/shard_map/all_to_all | solution.py:354
  135.1 8.8 %all-to-all-start.1 = ((bf16[8,216,128]{2,1,0:T(8,128)(2,1)}), bf16[8,216,128]{2,1,0:T(8,128)(2,1)S(1)}, u32[]{:S(2)}, u32[]{:S(2)}) async-start(bf16[8,216,128]{2,1,0:T(8,128)(2,1)} %broadcast_in_dim.6), calls=%async_computation.1 | async-start | bytes 884736 | tf_op jit(solution)/shard_map/all_to_all | solution.py:354
  143.8 8.8 %shard_map.80 = bf16[4,512,128]{2,1,0:T(8,128)(2,1)} custom-call(s32[4,26]{1,0:T(4,128)} %bitcast.34, s32[1]{0:T(128)} %bitcast.1.dev, bf16[4,512,128]{2,1,0:T(8,128)(2,1)} %get-tuple-element.59.hid, bf16[896,128]{1,0:T(8,128)(2,1)} %get-tuple-element.60.refs_0_, bf16[896,128]{1,0:T(8,128)(2,1)} %get-tuple-element.61.refs_1_, bf16[896,128]{1,0:T(8,128)(2,1)} %copy-done.6, ...), custom_call_target="tpu_custom_call" | custom-call | tf_op jit(solution)/shard_map/pallas_call | solution.py:319
  152.6 4.5 %all-to-all-done.1 = bf16[8,216,128]{2,1,0:T(8,128)(2,1)S(1)} async-done(((bf16[8,216,128]{2,1,0:T(8,128)(2,1)}), bf16[8,216,128]{2,1,0:T(8,128)(2,1)S(1)}, u32[]{:S(2)}, u32[]{:S(2)}) %all-to-all-start.1) | async-done | bytes 442400 | tf_op jit(solution)/shard_map/all_to_all | solution.py:354
  157.3 17.4 %all_to_all.16 = bf16[16,216,128]{2,1,0:T(8,128)(2,1)S(1)} all-to-all(bf16[16,216,128]{2,1,0:T(8,128)(2,1)S(1)} %broadcast_in_dim.8), channel_id=1, replica_groups={{0,1,2,3,64,65,66,67,128,129,130,131,192,193,194,195},{4,5,6,7,68,69,70..., dimensions={0} | all-to-all | bytes 1769472 | tf_op jit(solution)/shard_map/all_to_all | solution.py:354
  174.7 3.7 %collective-permute-start.19 = (bf16[3456,128]{1,0:T(8,128)(2,1)S(1)}, bf16[3456,128]{1,0:T(8,128)(2,1)S(1)}, u32[]{:S(2)}, u32[]{:S(2)}) collective-permute-start(bf16[3456,128]{1,0:T(8,128)(2,1)S(1)} %bitcast.18), channel_id=1, source_target_pairs={{0,4},{4,0},{8,12},{12,8},{16,20},{20,16},{24,28},{28,24},{32,36},... | collective-permute-start | bytes 2654216 | tf_op jit(solution)/shard_map/ppermute | solution.py:330
  178.5 2.1 %collective-permute-done.19 = bf16[3456,128]{1,0:T(8,128)(2,1)S(1)} collective-permute-done((bf16[3456,128]{1,0:T(8,128)(2,1)S(1)}, bf16[3456,128]{1,0:T(8,128)(2,1)S(1)}, u32[]{:S(2)}, u32[]{:S(2)}) %collective-permute-start.19) | collective-permute-done | bytes 884768 | tf_op jit(solution)/shard_map/ppermute | solution.py:330
  (86 shorter events, 20.1 us)
Async XLA Ops:
  3.3 18.1 %collective-permute-start = (bf16[1792,128]{1,0:T(8,128)(2,1)}, bf16[1792,128]{1,0:T(8,128)(2,1)S(1)}, u32[]{:S(2)}, u32[]{:S(2)}) collective-permute-start(bf16[1792,128]{1,0:T(8,128)(2,1)} %get-tuple-element.38.refs_0_), channel_id=1, source_target_pairs={{0,248},{4,252},{8,0},{12,4},{16,8},{20,12},{24,16},{28,20},{32,24... | collective-permute-start | bytes 1376264 | tf_op jit(solution)/shard_map/ppermute | solution.py:330
  11.9 15.0 %collective-permute-start.1 = (bf16[1792,128]{1,0:T(8,128)(2,1)}, bf16[1792,128]{1,0:T(8,128)(2,1)S(1)}, u32[]{:S(2)}, u32[]{:S(2)}) collective-permute-start(bf16[1792,128]{1,0:T(8,128)(2,1)} %get-tuple-element.39.refs_1_), channel_id=1, source_target_pairs={{0,8},{4,12},{8,16},{12,20},{16,24},{20,28},{24,32},{28,36},{32,40... | collective-permute-start | bytes 1376264 | tf_op jit(solution)/shard_map/ppermute | solution.py:330
  21.4 22.7 %collective-permute-start.2 = (bf16[768,128]{1,0:T(8,128)(2,1)S(1)}, bf16[768,128]{1,0:T(8,128)(2,1)S(1)}, u32[]{:S(2)}, u32[]{:S(2)}) collective-permute-start(bf16[768,128]{1,0:T(8,128)(2,1)S(1)} %slice.36), channel_id=1, source_target_pairs={{0,248},{4,252},{8,0},{12,4},{16,8},{20,12},{24,16},{28,20},{32,24... | collective-permute-start | bytes 589832 | tf_op jit(solution)/shard_map/ppermute | solution.py:330
  26.9 17.2 %collective-permute-start.3 = (bf16[768,128]{1,0:T(8,128)(2,1)S(1)}, bf16[768,128]{1,0:T(8,128)(2,1)S(1)}, u32[]{:S(2)}, u32[]{:S(2)}) collective-permute-start(bf16[768,128]{1,0:T(8,128)(2,1)S(1)} %slice.37), channel_id=1, source_target_pairs={{0,8},{4,12},{8,16},{12,20},{16,24},{20,28},{24,32},{28,36},{32,40... | collective-permute-start | bytes 589832 | tf_op jit(solution)/shard_map/ppermute | solution.py:330
  28.2 17.7 %copy-start.3 = (bf16[27,128,128]{2,1,0:T(8,128)(2,1)S(1)}, bf16[27,128,128]{2,1,0:T(8,128)(2,1)}, u32[]{:S(2)}) copy-start(bf16[27,128,128]{2,1,0:T(8,128)(2,1)} %param.7) | copy-start | bytes 2654212
  28.2 24.4 %collective-permute-start.7 = (bf16[5376,128]{1,0:T(8,128)(2,1)}, bf16[5376,128]{1,0:T(8,128)(2,1)S(1)}, u32[]{:S(2)}, u32[]{:S(2)}) collective-permute-start(bf16[5376,128]{1,0:T(8,128)(2,1)} %pad_maximum_fusion), channel_id=1, source_target_pairs={{0,4},{4,0},{8,12},{12,8},{16,20},{20,16},{24,28},{28,24},{32,36},... | collective-permute-start | bytes 4128776 | tf_op jit(solution)/shard_map/ppermute | solution.py:330
  30.7 7.9 %collective-permute-start.4 = (bf16[512,128]{1,0:T(8,128)(2,1)S(1)}, bf16[512,128]{1,0:T(8,128)(2,1)S(1)}, u32[]{:S(2)}, u32[]{:S(2)}) collective-permute-start(bf16[512,128]{1,0:T(8,128)(2,1)S(1)} %get-tuple-element.76), channel_id=1, source_target_pairs={{0,240},{4,244},{8,248},{12,252},{16,0},{20,4},{24,8},{28,12},{32,... | collective-permute-start | bytes 393224 | tf_op jit(solution)/shard_map/ppermute | solution.py:330
  31.9 12.2 %collective-permute-start.5 = (bf16[512,128]{1,0:T(8,128)(2,1)S(1)}, bf16[512,128]{1,0:T(8,128)(2,1)S(1)}, u32[]{:S(2)}, u32[]{:S(2)}) collective-permute-start(bf16[512,128]{1,0:T(8,128)(2,1)S(1)} %get-tuple-element.77), channel_id=1, source_target_pairs={{0,16},{4,20},{8,24},{12,28},{16,32},{20,36},{24,40},{28,44},{32,4... | collective-permute-start | bytes 393224 | tf_op jit(solution)/shard_map/ppermute | solution.py:330
  45.1 7.5 %collective-permute-start.8 = (bf16[2560,128]{1,0:T(8,128)(2,1)}, bf16[2560,128]{1,0:T(8,128)(2,1)}, u32[]{:S(2)}, u32[]{:S(2)}) collective-permute-start(bf16[2560,128]{1,0:T(8,128)(2,1)} %pad_maximum_fusion.2), channel_id=1, source_target_pairs={{0,4},{4,0},{8,12},{12,8},{16,20},{20,16},{24,28},{28,24},{32,36},... | collective-permute-start | bytes 1966088 | tf_op jit(solution)/shard_map/ppermute | solution.py:330
  45.9 6.7 %collective-permute-start.6 = (bf16[512,128]{1,0:T(8,128)(2,1)}, bf16[512,128]{1,0:T(8,128)(2,1)}, u32[]{:S(2)}, u32[]{:S(2)}) collective-permute-start(bf16[512,128]{1,0:T(8,128)(2,1)} %get-tuple-element.75), channel_id=1, source_target_pairs={{0,236},{4,24},{8,244},{12,32},{16,252},{20,40},{24,4},{28,48},{32... | collective-permute-start | bytes 393224 | tf_op jit(solution)/shard_map/ppermute | solution.py:330
  64.9 16.3 %collective-permute-start.9 = (bf16[896,128]{1,0:T(8,128)(2,1)}, bf16[896,128]{1,0:T(8,128)(2,1)S(1)}, u32[]{:S(2)}, u32[]{:S(2)}) collective-permute-start(bf16[896,128]{1,0:T(8,128)(2,1)} %get-tuple-element.60.refs_0_), channel_id=1, source_target_pairs={{0,248},{4,252},{8,0},{12,4},{16,8},{20,12},{24,16},{28,20},{32,24... | collective-permute-start | bytes 688136 | tf_op jit(solution)/shard_map/ppermute | solution.py:330
  70.7 10.5 %collective-permute-start.10 = (bf16[896,128]{1,0:T(8,128)(2,1)}, bf16[896,128]{1,0:T(8,128)(2,1)S(1)}, u32[]{:S(2)}, u32[]{:S(2)}) collective-permute-start(bf16[896,128]{1,0:T(8,128)(2,1)} %get-tuple-element.61.refs_1_), channel_id=1, source_target_pairs={{0,8},{4,12},{8,16},{12,20},{16,24},{20,28},{24,32},{28,36},{32,40... | collective-permute-start | bytes 688136 | tf_op jit(solution)/shard_map/ppermute | solution.py:330
  81.2 15.6 %copy-start.6 = (bf16[896,128]{1,0:T(8,128)(2,1)}, bf16[896,128]{1,0:T(8,128)(2,1)S(1)}, u32[]{:S(2)}) copy-start(bf16[896,128]{1,0:T(8,128)(2,1)S(1)} %collective-permute-done.9.refs_2_) | copy-start | bytes 688132
  81.3 15.5 %collective-permute-start.12 = (bf16[384,128]{1,0:T(8,128)(2,1)S(1)}, bf16[384,128]{1,0:T(8,128)(2,1)S(1)}, u32[]{:S(2)}, u32[]{:S(2)}) collective-permute-start(bf16[384,128]{1,0:T(8,128)(2,1)S(1)} %slice.33), channel_id=1, source_target_pairs={{0,8},{4,12},{8,16},{12,20},{16,24},{20,28},{24,32},{28,36},{32,40... | collective-permute-start | bytes 294920 | tf_op jit(solution)/shard_map/ppermute | solution.py:330
  82.2 14.5 %collective-permute-start.11 = (bf16[384,128]{1,0:T(8,128)(2,1)S(1)}, bf16[384,128]{1,0:T(8,128)(2,1)S(1)}, u32[]{:S(2)}, u32[]{:S(2)}) collective-permute-start(bf16[384,128]{1,0:T(8,128)(2,1)S(1)} %slice.32), channel_id=1, source_target_pairs={{0,248},{4,252},{8,0},{12,4},{16,8},{20,12},{24,16},{28,20},{32,24... | collective-permute-start | bytes 294920 | tf_op jit(solution)/shard_map/ppermute | solution.py:330
  86.5 23.7 %collective-permute-start.16 = (bf16[2688,128]{1,0:T(8,128)(2,1)S(1)}, bf16[2688,128]{1,0:T(8,128)(2,1)S(1)}, u32[]{:S(2)}, u32[]{:S(2)}) collective-permute-start(bf16[2688,128]{1,0:T(8,128)(2,1)S(1)} %pad_maximum_fusion.1), channel_id=1, source_target_pairs={{0,4},{4,0},{8,12},{12,8},{16,20},{20,16},{24,28},{28,24},{32,36},... | collective-permute-start | bytes 2064392 | tf_op jit(solution)/shard_map/ppermute | solution.py:330
  88.7 4.6 %collective-permute-start.13 = (bf16[256,128]{1,0:T(8,128)(2,1)S(1)}, bf16[256,128]{1,0:T(8,128)(2,1)S(1)}, u32[]{:S(2)}, u32[]{:S(2)}) collective-permute-start(bf16[256,128]{1,0:T(8,128)(2,1)S(1)} %get-tuple-element.79), channel_id=1, source_target_pairs={{0,240},{4,244},{8,248},{12,252},{16,0},{20,4},{24,8},{28,12},{32,... | collective-permute-start | bytes 196616 | tf_op jit(solution)/shard_map/ppermute | solution.py:330
  88.8 7.9 %collective-permute-start.14 = (bf16[256,128]{1,0:T(8,128)(2,1)S(1)}, bf16[256,128]{1,0:T(8,128)(2,1)S(1)}, u32[]{:S(2)}, u32[]{:S(2)}) collective-permute-start(bf16[256,128]{1,0:T(8,128)(2,1)S(1)} %get-tuple-element.80), channel_id=1, source_target_pairs={{0,16},{4,20},{8,24},{12,28},{16,32},{20,36},{24,40},{28,44},{32,4... | collective-permute-start | bytes 196616 | tf_op jit(solution)/shard_map/ppermute | solution.py:330
  93.3 16.8 %copy-start.16 = (bf16[256,128]{1,0:T(8,128)(2,1)}, bf16[256,128]{1,0:T(8,128)(2,1)S(1)}, u32[]{:S(2)}) copy-start(bf16[256,128]{1,0:T(8,128)(2,1)S(1)} %collective-permute-done.13.refs_6_) | copy-start | bytes 196612
  96.8 13.3 %collective-permute-start.17 = (bf16[1280,128]{1,0:T(8,128)(2,1)S(1)}, bf16[1280,128]{1,0:T(8,128)(2,1)S(1)}, u32[]{:S(2)}, u32[]{:S(2)}) collective-permute-start(bf16[1280,128]{1,0:T(8,128)(2,1)S(1)} %pad_maximum_fusion.3), channel_id=1, source_target_pairs={{0,4},{4,0},{8,12},{12,8},{16,20},{20,16},{24,28},{28,24},{32,36},... | collective-permute-start | bytes 983048 | tf_op jit(solution)/shard_map/ppermute | solution.py:330
  97.9 12.3 %collective-permute-start.15 = (bf16[256,128]{1,0:T(8,128)(2,1)S(1)}, bf16[256,128]{1,0:T(8,128)(2,1)S(1)}, u32[]{:S(2)}, u32[]{:S(2)}) collective-permute-start(bf16[256,128]{1,0:T(8,128)(2,1)S(1)} %get-tuple-element.78), channel_id=1, source_target_pairs={{0,236},{4,24},{8,244},{12,32},{16,252},{20,40},{24,4},{28,48},{32... | collective-permute-start | bytes 196616 | tf_op jit(solution)/shard_map/ppermute | solution.py:330
  110.2 4.0 %collective-permute-start.18 = (f32[3456,128]{1,0:T(8,128)}, f32[3456,128]{1,0:T(8,128)S(1)}, u32[]{:S(2)}, u32[]{:S(2)}) collective-permute-start(f32[3456,128]{1,0:T(8,128)} %get-tuple-element.56), channel_id=1, source_target_pairs={{0,4},{4,0},{8,12},{12,8},{16,20},{20,16},{24,28},{28,24},{32,36},... | collective-permute-start | bytes 5308424 | tf_op jit(solution)/shard_map/ppermute | solution.py:330
  135.1 22.1 %all-to-all-start.1 = ((bf16[8,216,128]{2,1,0:T(8,128)(2,1)}), bf16[8,216,128]{2,1,0:T(8,128)(2,1)S(1)}, u32[]{:S(2)}, u32[]{:S(2)}) async-start(bf16[8,216,128]{2,1,0:T(8,128)(2,1)} %broadcast_in_dim.6), calls=%async_computation.1 | async-start | bytes 884736 | tf_op jit(solution)/shard_map/all_to_all | solution.py:354
  174.7 5.8 %collective-permute-start.19 = (bf16[3456,128]{1,0:T(8,128)(2,1)S(1)}, bf16[3456,128]{1,0:T(8,128)(2,1)S(1)}, u32[]{:S(2)}, u32[]{:S(2)}) collective-permute-start(bf16[3456,128]{1,0:T(8,128)(2,1)S(1)} %bitcast.18), channel_id=1, source_target_pairs={{0,4},{4,0},{8,12},{12,8},{16,20},{20,16},{24,28},{28,24},{32,36},... | collective-permute-start | bytes 2654216 | tf_op jit(solution)/shard_map/ppermute | solution.py:330
  (16 other events, 119.7 us)
where the time goes:
time: 184 us; the launch traced here: 183 us
  starting transfers between devices  48.5 us (26%)
  Pallas kernels  45.3 us (25%)
  waiting for transfers between devices  40.4 us (22%)
  blocking collectives  35.6 us (19%)
  other arithmetic  8.92 us (5%)
  local copies, waits for them, and re-layouts  3.86 us (2%)
    pallas_call x5, Pallas kernels, call(): pl.pallas_call(kernel, out_shape=[jax.ShapeDtypeStruct(shape, dtype) for...  45.3 us
    ppermute x20, starting transfers between devices, hop(): lax.ppermute(x, 'blocks', [(i, (i + shift(i)) % size) for i in range(size)])  39.7 us
    ppermute x20, waiting for transfers between devices, hop(): lax.ppermute(x, 'blocks', [(i, (i + shift(i)) % size) for i in range(size)])  35.9 us
    all_to_all x2, blocking collectives, all_to_all(): return lax.all_to_all(x, axes, 0, 0, axis_index_groups=groups, tiled=True)  35.6 us
    all_to_all x1, starting transfers between devices, all_to_all(): return lax.all_to_all(x, axes, 0, 0, axis_index_groups=groups, tiled=True)  8.78 us
    all_to_all x1, waiting for transfers between devices, all_to_all(): return lax.all_to_all(x, axes, 0, 0, axis_index_groups=groups, tiled=True)  4.48 us
  transfers between devices with their start and end apart: 21, of which 9 were waited for; matrix products, arithmetic and copies ran while one was open for 3% of the time, Pallas kernels for 17%

commit v1 on v0

--- a/solution.py
+++ b/solution.py
@@ -26,10 +26,8 @@
 F32 = jnp.float32
 
 
-def pack_field(nb, dev, own, down, up, fields, f):
-    ox, oe = f * RX, fields * RX + f * RE
-    oj = fields * (RX + RE) + f * RP
-    ol = fields * (RX + RE + RP) + f * RP
+def pack_field(nb, dev, own, down, up):
+    ox, oe, oj, ol = 0, RX, RX + RE, RX + RE + RP
 
     def body(b, carry):
         me = dev * BD + b
@@ -60,9 +58,8 @@
     lax.fori_loop(0, BD, body, 0)
 
 
-def fill_tables(core, pieces, tx, te, tj, tl, fields, f):
-    own_down, own_up, d1, u1, d2, u2, d3, u3, v4, near, wide = pieces
-    full, mid, far = fields * FULL, fields * MID, fields * FAR
+def fill_tables(core, pieces, tx, te, tj, tl):
+    own_down, own_up, d1, u1, d2, u2, v4, near, wide_d, wide_u = pieces
     turn = 2 * core
     plan = [
         (own_down, 0, 10, 4),
@@ -71,27 +68,26 @@
         (u1, 0, 7, 4),
         (d2, 0, 14, 2),
         (u2, 0, 5, 2),
-        (d3, 0, 16, 1),
-        (u3, 0, 3, 1),
+        (d2, MID, 16, 1),
+        (u2, MID, 3, 1),
         (v4, 0, 2 + 15 * core, 1),
         (near, 0, 11 - 3 * core, 4),
-        (near, full, 13 - turn, 4),
-        (near, 2 * full, 8 - turn, 4),
-        (wide, 0, 15 - turn, 2),
-        (wide, mid, 6 - turn, 2),
-        (wide, 2 * mid, 17 - turn, 1),
-        (wide, 2 * mid + far, 4 - turn, 1),
+        (near, FULL, 13 - turn, 4),
+        (near, 2 * FULL, 8 - turn, 4),
+        (wide_d, 0, 15 - turn, 2),
+        (wide_u, 0, 6 - turn, 2),
+        (wide_d, MID, 17 - turn, 1),
+        (wide_u, MID, 4 - turn, 1),
     ]
-    for ref, base, slot, kind in plan:
-        row = base + f * RX
+    for ref, row, slot, kind in plan:
         tx[slot] = ref[row : row + RX, :].astype(F32).reshape(BD, 64, CH)
         if kind >= 2:
-            row = base + fields * RX + f * RE
+            row += RX
             te[slot] = ref[row : row + RE, :].astype(F32).reshape(BD, 32, CH)
         if kind >= 4:
-            row = base + fields * (RX + RE) + f * RP
+            row += RE
             tj[slot] = ref[row : row + RP, :].astype(F32).reshape(BD, 64, CH)
-            row += fields * RP
+            row += RP
             tl[slot] = ref[row : row + RP, :].astype(F32).reshape(BD, 64, CH)
 
 
@@ -196,17 +192,16 @@
         own[b] = ref[b].astype(F32)
 
 
-def pack_kernel(nb, dev, feat, cot, down, up, own):
-    for f, ref in enumerate((feat, cot)):
-        load_own(ref, own)
-        pack_field(nb, dev[0], own, down, up, 2, f)
+def pack_kernel(nb, dev, field, down, up, own):
+    load_own(field, own)
+    pack_field(nb, dev[0], own, down, up)
 
 
 def forward_kernel(nb, dev, feat, *refs):
-    pieces, weight = refs[:11], refs[11]
-    hid, hid_s, pre, down, up, sh, own, tx, te, tj, tl, cf, lf, rf = refs[12:]
+    pieces, weight = refs[:10], refs[10]
+    hid, hid_s, pre, down, up, sh, own, tx, te, tj, tl, cf, lf, rf = refs[11:]
     load_own(feat, own)
-    fill_tables(dev[0] & 1, pieces, tx, te, tj, tl, 2, 0)
+    fill_tables(dev[0] & 1, pieces, tx, te, tj, tl)
     build_shifted(nb, dev[0], own, tx, te, tj, tl, cf, lf, rf, sh)
 
     def emit(pair, first, rows):
@@ -222,14 +217,14 @@
         split_blocks(pair, first, act.astype(F32), store)
 
     conv(sh, weight, emit)
-    pack_field(nb, dev[0], own, down, up, 1, 0)
+    pack_field(nb, dev[0], own, down, up)
 
 
 def backward_kernel(nb, dev, cot, *refs):
-    pieces, weight, hid_s, pre = refs[:11], refs[11], refs[12], refs[13]
-    sh, hid_t, delta_t, own, tx, te, tj, tl, cf, lf, rf, delta = refs[14:]
+    pieces, weight, hid_s, pre = refs[:10], refs[10], refs[11], refs[12]
+    sh, hid_t, delta_t, own, tx, te, tj, tl, cf, lf, rf, delta = refs[13:]
     load_own(cot, own)
-    fill_tables(dev[0] & 1, pieces, tx, te, tj, tl, 2, 1)
+    fill_tables(dev[0] & 1, pieces, tx, te, tj, tl)
     build_shifted(nb, dev[0], own, tx, te, tj, tl, cf, lf, rf, sh)
 
     def emit(pair, first, rows):
@@ -240,33 +235,35 @@
 
     conv(sh, weight, emit)
     for pair in range(2):
-        hid_t[pair] = hid_s[pair * 1024 : pair * 1024 + 1024, :].T
-        delta_t[pair] = delta[pair * 1024 : pair * 1024 + 1024, :].T
+        at = slice(pair * 1024, pair * 1024 + 1024)
+        hid_t[:, at] = hid_s[at, :].T
+        delta_t[:, at] = delta[at, :].T
 
 
 def gradient_kernel(nb, dev, hid_t, delta_t, sh_feat, sh, keep, send):
-    def body(step, carry):
-        a, b = step // 3, step % 3
-
+    def body(a, carry):
         def product(left, ref):
-            total = None
-            for pair in range(2):
-                right = jnp.concatenate(
-                    [ref[c, pair, pl.ds(a, 8), pl.ds(b, 8)].reshape(1024, CH) for c in range(3)], axis=1
-                )
-                term = jnp.dot(left[pair], right, preferred_element_type=F32)
-                total = term if total is None else total + term
-            return total
-
-        one = product(delta_t, sh_feat)
-        two = product(hid_t, sh)
+            right = jnp.concatenate(
+                [
+                    jnp.concatenate(
+                        [ref[c, pair, pl.ds(a, 8), b : b + 8].reshape(1024, CH) for b in range(3) for c in range(3)],
+                        axis=1,
+                    )
+                    for pair in range(2)
+                ],
+                axis=0,
+            )
+            return jnp.dot(left[...], right, preferred_element_type=F32)
 
         def write(first, second):
-            for c in range(3):
-                row = pl.multiple_of((step * 3 + c) * CH, CH)
-                first[pl.ds(row, CH), :] = one[:, c * CH : c * CH + CH].T
-                row = pl.multiple_of((26 - step * 3 - c) * CH, CH)
-                second[pl.ds(row, CH), :] = two[:, c * CH : c * CH + CH]
+            one = product(delta_t, sh_feat)
+            for t in range(9):
+                row = pl.multiple_of((a * 9 + t) * CH, CH)
+                first[pl.ds(row, CH), :] = one[:, t * CH : t * CH + CH].T
+            two = product(hid_t, sh)
+            for t in range(9):
+                row = pl.multiple_of((26 - a * 9 - t) * CH, CH)
+                second[pl.ds(row, CH), :] = two[:, t * CH : t * CH + CH]
 
         @pl.when((dev[0] & 1) == 0)
         def _():
@@ -278,14 +275,14 @@
 
         return carry
 
-    lax.fori_loop(0, 9, body, 0)
+    lax.fori_loop(0, 3, body, 0)
 
 
 def second_kernel(nb, dev, hid, *refs):
-    pieces, weight, out = refs[:11], refs[11], refs[12]
-    own, tx, te, tj, tl, cf, lf, rf, sh = refs[13:]
+    pieces, weight, out = refs[:10], refs[10], refs[11]
+    own, tx, te, tj, tl, cf, lf, rf, sh = refs[12:]
     load_own(hid, own)
-    fill_tables(dev[0] & 1, pieces, tx, te, tj, tl, 1, 0)
+    fill_tables(dev[0] & 1, pieces, tx, te, tj, tl)
     build_shifted(nb, dev[0], own, tx, te, tj, tl, cf, lf, rf, sh)
 
     def emit(pair, first, rows):
@@ -311,9 +308,10 @@
 
 
 SHIFTED = (3, 2, 10, 10, 16, CH)
-
-
-def call(kernel, outs, scratch, nb, dev, *arrays):
+LIMIT = 36
+
+
+def call(kernel, outs, scratch, nb, dev, *arrays, limit=LIMIT):
     smem = pl.BlockSpec(memory_space=pltpu.SMEM)
     vmem = pl.BlockSpec(memory_space=pltpu.VMEM)
     return pl.pallas_call(
@@ -322,6 +320,7 @@
         in_specs=[smem, smem] + [vmem] * len(arrays),
         out_specs=[vmem] * len(outs),
         scratch_shapes=scratch,
+        compiler_params=pltpu.CompilerParams(vmem_limit_bytes=limit << 20),
     )(nb, dev, *arrays)
 
 
@@ -338,16 +337,36 @@
     return hop(down, lambda i: -2), hop(up, lambda i: 2)
 
 
-def exchange_rest(down, up, d1, u1, fields, core):
-    mid, far = fields * MID, fields * FAR
-    last = jnp.where(core == 0, d1[:far], u1[:far])
+def forward_planes(nb, dev, down, up, d1, u1, far_down, far_up, last, near):
+    for own, got, out in ((down, d1, far_down), (up, u1, far_up)):
+        out[0:MID, :] = own[0:MID, :]
+        out[MID : MID + FAR, :] = got[0:FAR, :]
+    near[FULL : 2 * FULL, :] = d1[...]
+    near[2 * FULL : 3 * FULL, :] = u1[...]
+    first = (dev[0] & 1) == 0
+
+    @pl.when(first)
+    def _():
+        last[...] = d1[0:FAR, :]
+        near[0:FULL, :] = up[...]
+
+    @pl.when(jnp.logical_not(first))
+    def _():
+        last[...] = u1[0:FAR, :]
+        near[0:FULL, :] = down[...]
+
+
+def exchange_far(nb, dev, down, up, d1, u1):
+    outs = [((MID + FAR, CH), BF)] * 2 + [((FAR, CH), BF), ((3 * FULL, CH), BF)]
+    far_down, far_up, last, near = call(forward_planes, outs, [], nb, dev, down, up, d1, u1, limit=8)
     v4 = hop(last, lambda i: -5 if i % 2 == 0 else 5)
-    d3, u3 = hop(d1[:far], lambda i: -4), hop(u1[:far], lambda i: 4)
-    d2, u2 = hop(d1[:mid], lambda i: -2), hop(u1[:mid], lambda i: 2)
-    mine = jnp.where(core == 0, up, down)
-    near = swap(jnp.concatenate([mine, d1, u1], axis=0))
-    wide = swap(jnp.concatenate([d2, u2, d3, u3], axis=0))
-    return (down, up, d1, u1, d2, u2, d3, u3, v4, near, wide)
+    d2 = hop(far_down, lambda i: -4)
+    u2 = hop(far_up, lambda i: 4)
+    return d2, u2, v4, swap(near)
+
+
+def exchange_wide(d2, u2):
+    return swap(d2), swap(u2)
 
 
 def all_to_all(x, axes, groups):
@@ -395,10 +414,15 @@
     w_one = weight_one.reshape(27 * CH, CH)
     w_two = weight_two.reshape(27 * CH, CH)
     flipped = jnp.transpose(weight_two[::-1], (0, 2, 1)).reshape(27 * CH, CH)
-    two_fields = (2 * FULL, CH)
-    down, up = call(pack_kernel, [(two_fields, BF)] * 2, scratch_own(), nb, dev, feat, cot)
-    d1, u1 = exchange_near(down, up)
-    pieces = exchange_rest(down, up, d1, u1, 2, core)
+    halo = [((FULL, CH), BF)] * 2
+    f_down, f_up = call(pack_kernel, halo, scratch_own(), nb, dev, feat)
+    f_d1, f_u1 = exchange_near(f_down, f_up)
+    c_down, c_up = call(pack_kernel, halo, scratch_own(), nb, dev, cot)
+    c_d1, c_u1 = exchange_near(c_down, c_up)
+    f_d1, f_u1, flipped = lax.optimization_barrier((f_d1, f_u1, flipped))
+    f_far = exchange_far(nb, dev, f_down, f_up, f_d1, f_u1)
+    c_far = exchange_far(nb, dev, c_down, c_up, c_d1, c_u1)
+    pieces = (f_down, f_up, f_d1, f_u1, *f_far, *exchange_wide(f_far[0], f_far[1]))
     hid, hid_s, pre, hid_down, hid_up, sh_feat = call(
         forward_kernel,
         [
@@ -416,10 +440,12 @@
         *pieces,
         w_one,
     )
+    c_far, hid_down, hid_up = lax.optimization_barrier((c_far, hid_down, hid_up))
     d1, u1 = exchange_near(hid_down, hid_up)
+    pieces = (c_down, c_up, c_d1, c_u1, *c_far, *exchange_wide(c_far[0], c_far[1]))
     sh_cot, hid_t, delta_t = call(
         backward_kernel,
-        [(SHIFTED, BF), ((2, CH, 1024), BF), ((2, CH, 1024), BF)],
+        [(SHIFTED, BF), ((CH, BD * 512), BF), ((CH, BD * 512), BF)],
         scratch_own() + scratch_build() + [pltpu.VMEM((BD * 512, CH), BF)],
         nb,
         dev,
@@ -430,7 +456,7 @@
         pre,
     )
     d1, u1, hid_t, delta_t, sh_cot = lax.optimization_barrier((d1, u1, hid_t, delta_t, sh_cot))
-    hid_pieces = exchange_rest(hid_down, hid_up, d1, u1, 1, core)
+    h_far = exchange_far(nb, dev, hid_down, hid_up, d1, u1)
     keep, send = call(
         gradient_kernel,
         [((27 * CH, CH), F32)] * 2,
@@ -442,7 +468,8 @@
         sh_feat,
         sh_cot,
     )
-    (keep, send), hid_pieces = lax.optimization_barrier(((keep, send), hid_pieces))
+    (keep, send), h_far = lax.optimization_barrier(((keep, send), h_far))
+    hid_pieces = (hid_down, hid_up, d1, u1, *h_far, *exchange_wide(h_far[0], h_far[1]))
     voxel_total = lax.axis_size("rep") * lax.axis_size("blocks") * BD * 512
     scale = 1.0 / math.sqrt(voxel_total)
 

time: 184 us -> 168 us (0.913)
  Pallas kernels: 45.3 us -> 29.5 us
  waiting for transfers between devices: 40.4 us -> 32.2 us
  starting transfers between devices: 48.5 us -> 54.8 us
  local copies, waits for them, and re-layouts: 3.86 us -> 8.65 us
  other arithmetic: 8.92 us -> 5.55 us
    pallas_call x5 -> x9, Pallas kernels: 45.3 us -> 29.5 us  [call(): pl.pallas_call(kernel, out_shape=[jax.ShapeDtypeStruct(shape, dtype) for...]
    ppermute x20 -> x26, starting transfers between devices: 39.7 us -> 46.7 us  [hop(): lax.ppermute(x, 'blocks', [(i, (i + shift(i)) % size) for i in range(size)])]
    ppermute x20 -> x26, waiting for transfers between devices: 35.9 us -> 30.5 us  [hop(): lax.ppermute(x, 'blocks', [(i, (i + shift(i)) % size) for i in range(size)])]
    all_to_all x1, waiting for transfers between devices: 4.48 us -> 1.65 us  [all_to_all(): return lax.all_to_all(x, axes, 0, 0, axis_index_groups=groups, tiled=True)]
    unnamed x38 -> x24, local copies, waits for them, and re-layouts: 1.15 us -> 3.59 us
    transpose x2, local copies, waits for them, and re-layouts: 1.74 us -> 4.12 us  [slab_step(): flipped = jnp.transpose(weight_two[::-1], (0, 2, 1)).reshape(27 * CH, CH)]
    concatenate x4 -> x0, other arithmetic: 2.18 us -> none  [the longest x2 1.21 us: exchange_rest(): near = swap(jnp.concatenate([mine, d1, u1], axis=0))]
  transfers between devices with their start and end apart: 21 -> 27, of which waited for: 9 -> 15; matrix products, arithmetic and copies ran while one was open for 3% -> 2% of each run, Pallas kernels for 17% -> 17%
where the time goes in v1:
time: 168 us; the launch traced here: 167 us
  starting transfers between devices  54.8 us (33%)
  blocking collectives  35.7 us (21%)
  waiting for transfers between devices  32.2 us (19%)
  Pallas kernels  29.5 us (18%)
  local copies, waits for them, and re-layouts  8.65 us (5%)
  other arithmetic  5.55 us (3%)
    ppermute x26, starting transfers between devices, hop(): lax.ppermute(x, 'blocks', [(i, (i + shift(i)) % size) for i in range(size)])  46.7 us
    all_to_all x2, blocking collectives, all_to_all(): return lax.all_to_all(x, axes, 0, 0, axis_index_groups=groups, tiled=True)  35.7 us
    ppermute x26, waiting for transfers between devices, hop(): lax.ppermute(x, 'blocks', [(i, (i + shift(i)) % size) for i in range(size)])  30.5 us
    pallas_call x9, Pallas kernels, call(): pl.pallas_call(kernel, out_shape=[jax.ShapeDtypeStruct(shape, dtype) for...  29.5 us
    all_to_all x1, starting transfers between devices, all_to_all(): return lax.all_to_all(x, axes, 0, 0, axis_index_groups=groups, tiled=True)  8.04 us
    transpose x2, local copies, waits for them, and re-layouts, slab_step(): flipped = jnp.transpose(weight_two[::-1], (0, 2, 1)).reshape(27 * CH, CH)  4.12 us
    unnamed x24, local copies, waits for them, and re-layouts  3.59 us
  transfers between devices with their start and end apart: 27, of which 15 were waited for; matrix products, arithmetic and copies ran while one was open for 2% of the time, Pallas kernels for 17%

profile of v1, /device:TPU:1, one launch (start us, length us, event | category | flops | bytes accessed | tf_op | source)
XLA Modules:
  0.0 167.2 jit_solution(17334109627801008407)
XLA Ops:
  3.1 8.7 %collective-permute-start.6 = (bf16[896,128]{1,0:T(8,128)(2,1)S(1)}, bf16[896,128]{1,0:T(8,128)(2,1)S(1)}, u32[]{:S(2)}, u32[]{:S(2)}) collective-permute-start(bf16[896,128]{1,0:T(8,128)(2,1)S(1)} %get-tuple-element.60.down.refs_0_), channel_id=1, source_target_pairs={{0,248},{4,252},{8,0},{12,4},{16,8},{20,12},{24,16},{28,20},{32,24... | collective-permute-start | bytes 688136 | tf_op jit(solution)/shard_map/ppermute | solution.py:329
  13.6 4.9 %collective-permute-start = (bf16[896,128]{1,0:T(8,128)(2,1)S(1)}, bf16[896,128]{1,0:T(8,128)(2,1)S(1)}, u32[]{:S(2)}, u32[]{:S(2)}) collective-permute-start(bf16[896,128]{1,0:T(8,128)(2,1)S(1)} %get-tuple-element.54.down.refs_0_), channel_id=1, source_target_pairs={{0,248},{4,252},{8,0},{12,4},{16,8},{20,12},{24,16},{28,20},{32,24... | collective-permute-start | bytes 688136 | tf_op jit(solution)/shard_map/ppermute | solution.py:329
  24.9 2.5 %collective-permute-done.1.u1.refs_3_ = bf16[896,128]{1,0:T(8,128)(2,1)S(1)} collective-permute-done((bf16[896,128]{1,0:T(8,128)(2,1)S(1)}, bf16[896,128]{1,0:T(8,128)(2,1)S(1)}, u32[]{:S(2)}, u32[]{:S(2)}) %collective-permute-start.1) | collective-permute-done | bytes 229408 | tf_op jit(solution)/shard_map/ppermute | solution.py:329
  28.1 2.5 %collective-permute-start.5 = (bf16[2688,128]{1,0:T(8,128)(2,1)S(1)}, bf16[2688,128]{1,0:T(8,128)(2,1)S(1)}, u32[]{:S(2)}, u32[]{:S(2)}) collective-permute-start(bf16[2688,128]{1,0:T(8,128)(2,1)S(1)} %get-tuple-element.59), channel_id=1, source_target_pairs={{0,4},{4,0},{8,12},{12,8},{16,20},{20,16},{24,28},{28,24},{32,36},... | collective-permute-start | bytes 2064392 | tf_op jit(solution)/shard_map/ppermute | solution.py:329
  30.6 2.4 %collective-permute-start.9 = (bf16[640,128]{1,0:T(8,128)(2,1)S(1)}, bf16[640,128]{1,0:T(8,128)(2,1)S(1)}, u32[]{:S(2)}, u32[]{:S(2)}) collective-permute-start(bf16[640,128]{1,0:T(8,128)(2,1)S(1)} %get-tuple-element.65), channel_id=1, source_target_pairs={{0,16},{4,20},{8,24},{12,28},{16,32},{20,36},{24,40},{28,44},{32,4... | collective-permute-start | bytes 491528 | tf_op jit(solution)/shard_map/ppermute | solution.py:329
  33.0 5.7 %collective-permute-done.8.refs_4_ = bf16[640,128]{1,0:T(8,128)(2,1)S(1)} collective-permute-done((bf16[640,128]{1,0:T(8,128)(2,1)S(1)}, bf16[640,128]{1,0:T(8,128)(2,1)S(1)}, u32[]{:S(2)}, u32[]{:S(2)}) %collective-permute-start.8) | collective-permute-done | bytes 163872 | tf_op jit(solution)/shard_map/ppermute | solution.py:329
  39.7 2.2 %collective-permute-done.9.refs_5_ = bf16[640,128]{1,0:T(8,128)(2,1)S(1)} collective-permute-done((bf16[640,128]{1,0:T(8,128)(2,1)S(1)}, bf16[640,128]{1,0:T(8,128)(2,1)S(1)}, u32[]{:S(2)}, u32[]{:S(2)}) %collective-permute-start.9) | collective-permute-done | bytes 163872 | tf_op jit(solution)/shard_map/ppermute | solution.py:329
  43.0 3.9 %collective-permute-done.10.refs_6_ = bf16[256,128]{1,0:T(8,128)(2,1)S(1)} collective-permute-done((bf16[256,128]{1,0:T(8,128)(2,1)S(1)}, bf16[256,128]{1,0:T(8,128)(2,1)S(1)}, u32[]{:S(2)}, u32[]{:S(2)}) %collective-permute-start.10) | collective-permute-done | bytes 65568 | tf_op jit(solution)/shard_map/ppermute | solution.py:329
  46.9 6.0 %collective-permute-start.2 = (bf16[640,128]{1,0:T(8,128)(2,1)S(1)}, bf16[640,128]{1,0:T(8,128)(2,1)S(1)}, u32[]{:S(2)}, u32[]{:S(2)}) collective-permute-start(bf16[640,128]{1,0:T(8,128)(2,1)S(1)} %get-tuple-element.56), channel_id=1, source_target_pairs={{0,240},{4,244},{8,248},{12,252},{16,0},{20,4},{24,8},{28,12},{32,... | collective-permute-start | bytes 491528 | tf_op jit(solution)/shard_map/ppermute | solution.py:329
  53.0 6.7 %shard_map.80 = (bf16[4,512,128]{2,1,0:T(8,128)(2,1)S(1)}, bf16[2048,128]{1,0:T(8,128)(2,1)S(1)}, f32[2048,128]{1,0:T(8,128)S(1)}, bf16[896,128]{1,0:T(8,128)(2,...) custom-call(s32[4,26]{1,0:T(4,128)S(1)} %bitcast.29, s32[1]{0:T(128)} %bitcast.1.dev, ...), custom_call_target="tpu_custom_call" | custom-call | tf_op jit(solution)/shard_map/pallas_call | solution.py:317
  60.5 5.4 %collective-permute-done.3.refs_5_ = bf16[640,128]{1,0:T(8,128)(2,1)S(1)} collective-permute-done((bf16[640,128]{1,0:T(8,128)(2,1)S(1)}, bf16[640,128]{1,0:T(8,128)(2,1)S(1)}, u32[]{:S(2)}, u32[]{:S(2)}) %collective-permute-start.3) | collective-permute-done | bytes 163872 | tf_op jit(solution)/shard_map/ppermute | solution.py:329
  66.0 2.8 %collective-permute-start.14 = (bf16[896,128]{1,0:T(8,128)(2,1)S(1)}, bf16[896,128]{1,0:T(8,128)(2,1)S(1)}, u32[]{:S(2)}, u32[]{:S(2)}) collective-permute-start(bf16[896,128]{1,0:T(8,128)(2,1)S(1)} %get-tuple-element.70.down.refs_0_), channel_id=1, source_target_pairs={{0,248},{4,252},{8,0},{12,4},{16,8},{20,12},{24,16},{28,20},{32,24... | collective-permute-start | bytes 688136 | tf_op jit(solution)/shard_map/ppermute | solution.py:329
  70.5 6.8 %shard_map.81 = (bf16[3,2,10,10,16,128]{5,4,3,2,1,0:T(8,128)(2,1)S(1)}, bf16[128,2048]{1,0:T(8,128)(2,1)S(1)}, bf16[128,2048]{1,0:T(8,128)(2,1)S(1)}) custom-call(s32[4,26]{1,0:T(4,128)S(1)} %bitcast.30, s32[1]{0:T(128)} %bitcast.1.dev, bf16[4,512,128]{2,1,0:T(8,128)(2,1)S(1)} %bitcast.23, bf16[896,128]{1,0:T(8,128)(2,1)S(1)} %get-tuple-element.54.down.refs_0_, ...), custom_call_target="tpu_custom_call" | custom-call | tf_op jit(solution)/shard_map/pallas_call | solution.py:317
  79.5 2.8 %collective-permute-start.19 = (bf16[640,128]{1,0:T(8,128)(2,1)S(1)}, bf16[640,128]{1,0:T(8,128)(2,1)S(1)}, u32[]{:S(2)}, u32[]{:S(2)}) collective-permute-start(bf16[640,128]{1,0:T(8,128)(2,1)S(1)} %get-tuple-element.91), channel_id=1, source_target_pairs={{0,16},{4,20},{8,24},{12,28},{16,32},{20,36},{24,40},{28,44},{32,4... | collective-permute-start | bytes 491528 | tf_op jit(solution)/shard_map/ppermute | solution.py:329
  82.3 3.7 %collective-permute-start.20 = (bf16[256,128]{1,0:T(8,128)(2,1)S(1)}, bf16[256,128]{1,0:T(8,128)(2,1)S(1)}, u32[]{:S(2)}, u32[]{:S(2)}) collective-permute-start(bf16[256,128]{1,0:T(8,128)(2,1)S(1)} %get-tuple-element.92), channel_id=1, source_target_pairs={{0,236},{4,24},{8,244},{12,32},{16,252},{20,40},{24,4},{28,48},{32... | collective-permute-start | bytes 196616 | tf_op jit(solution)/shard_map/ppermute | solution.py:329
  86.0 5.3 %shard_map.82 = (f32[3456,128]{1,0:T(8,128)S(1)}, f32[3456,128]{1,0:T(8,128)S(1)}) custom-call(s32[4,26]{1,0:T(4,128)S(1)} %bitcast.32, s32[1]{0:T(128)} %bitcast.1.dev, bf16[128,2048]{1,0:T(8,128)(2,1)S(1)} %get-tuple-element.82.hid_t, bf16[128,2048]{1,0:T(8,128)(2,1)S(1)} %get-tuple-element.83.delta_t, ...), custom_call_target="tpu_custom_call" | custom-call | tf_op jit(solution)/shard_map/pallas_call | solution.py:317
  91.7 2.5 %collective-permute-done.19.refs_5_ = bf16[640,128]{1,0:T(8,128)(2,1)S(1)} collective-permute-done((bf16[640,128]{1,0:T(8,128)(2,1)S(1)}, bf16[640,128]{1,0:T(8,128)(2,1)S(1)}, u32[]{:S(2)}, u32[]{:S(2)}) %collective-permute-start.19) | collective-permute-done | bytes 163872 | tf_op jit(solution)/shard_map/ppermute | solution.py:329
  94.8 3.3 %collective-permute-done.22 = f32[3456,128]{1,0:T(8,128)S(1)} collective-permute-done((f32[3456,128]{1,0:T(8,128)S(1)}, f32[3456,128]{1,0:T(8,128)S(1)}, u32[]{:S(2)}, u32[]{:S(2)}) %collective-permute-start.22) | collective-permute-done | bytes 1769504 | tf_op jit(solution)/shard_map/ppermute | solution.py:329
  98.3 18.1 %all_to_all.15 = bf16[16,216,128]{2,1,0:T(8,128)(2,1)} all-to-all(bf16[16,216,128]{2,1,0:T(8,128)(2,1)S(1)} %bitcast.37), channel_id=1, replica_groups={{0,1,2,3,64,65,66,67,128,129,130,131,192,193,194,195},{4,5,6,7,68,69,70..., dimensions={0} | all-to-all | bytes 1769472 | tf_op jit(solution)/shard_map/all_to_all | solution.py:373
  118.5 8.0 %all-to-all-start.1 = ((bf16[8,216,128]{2,1,0:T(8,128)(2,1)}), bf16[8,216,128]{2,1,0:T(8,128)(2,1)}, u32[]{:S(2)}, u32[]{:S(2)}) async-start(bf16[8,216,128]{2,1,0:T(8,128)(2,1)} %broadcast_in_dim.6), calls=%async_computation.1 | async-start | bytes 884736 | tf_op jit(solution)/shard_map/all_to_all | solution.py:373
  126.6 2.6 %collective-permute-start.23 = (bf16[640,128]{1,0:T(8,128)(2,1)S(1)}, bf16[640,128]{1,0:T(8,128)(2,1)S(1)}, u32[]{:S(2)}, u32[]{:S(2)}) collective-permute-start(bf16[640,128]{1,0:T(8,128)(2,1)S(1)} %collective-permute-done.18.refs_4_), channel_id=1, source_target_pairs={{0,4},{4,0},{8,12},{12,8},{16,20},{20,16},{24,28},{28,24},{32,36},... | collective-permute-start | bytes 491528 | tf_op jit(solution)/shard_map/ppermute | solution.py:329
  130.6 7.2 %shard_map.84 = bf16[4,512,128]{2,1,0:T(8,128)(2,1)} custom-call(s32[4,26]{1,0:T(4,128)S(1)} %bitcast.33, s32[1]{0:T(128)} %bitcast.1.dev, bf16[4,512,128]{2,1,0:T(8,128)(2,1)S(1)} %copy-done.9, bf16[896,128]{1,0:T(8,128)(2,1)S(1)} %get-tuple-element.70.down.refs_0_, bf16[896,128]{1,0:T(8,128)(2,1)S(1)} %get-tuple-element.71.up.refs_1_, ...), custom_call_target="tpu_custom_call" | custom-call | tf_op jit(solution)/shard_map/pallas_call | solution.py:317
  140.7 17.6 %all_to_all.16 = bf16[16,216,128]{2,1,0:T(8,128)(2,1)S(1)} all-to-all(bf16[16,216,128]{2,1,0:T(8,128)(2,1)S(1)} %broadcast_in_dim.8), channel_id=1, replica_groups={{0,1,2,3,64,65,66,67,128,129,130,131,192,193,194,195},{4,5,6,7,68,69,70..., dimensions={0} | all-to-all | bytes 1769472 | tf_op jit(solution)/shard_map/all_to_all | solution.py:373
  158.3 3.9 %collective-permute-start.25 = (bf16[3456,128]{1,0:T(8,128)(2,1)S(1)}, bf16[3456,128]{1,0:T(8,128)(2,1)S(1)}, u32[]{:S(2)}, u32[]{:S(2)}) collective-permute-start(bf16[3456,128]{1,0:T(8,128)(2,1)S(1)} %bitcast.34), channel_id=1, source_target_pairs={{0,4},{4,0},{8,12},{12,8},{16,20},{20,16},{24,28},{28,24},{32,36},... | collective-permute-start | bytes 2654216 | tf_op jit(solution)/shard_map/ppermute | solution.py:329
  (76 shorter events, 30.9 us)
Async XLA Ops:
  3.1 19.5 %collective-permute-start.6 = (bf16[896,128]{1,0:T(8,128)(2,1)S(1)}, bf16[896,128]{1,0:T(8,128)(2,1)S(1)}, u32[]{:S(2)}, u32[]{:S(2)}) collective-permute-start(bf16[896,128]{1,0:T(8,128)(2,1)S(1)} %get-tuple-element.60.down.refs_0_), channel_id=1, source_target_pairs={{0,248},{4,252},{8,0},{12,4},{16,8},{20,12},{24,16},{28,20},{32,24... | collective-permute-start | bytes 688136 | tf_op jit(solution)/shard_map/ppermute | solution.py:329
  11.8 10.8 %collective-permute-start.7 = (bf16[896,128]{1,0:T(8,128)(2,1)S(1)}, bf16[896,128]{1,0:T(8,128)(2,1)S(1)}, u32[]{:S(2)}, u32[]{:S(2)}) collective-permute-start(bf16[896,128]{1,0:T(8,128)(2,1)S(1)} %get-tuple-element.61.up.refs_1_), channel_id=1, source_target_pairs={{0,8},{4,12},{8,16},{12,20},{16,24},{20,28},{24,32},{28,36},{32,40... | collective-permute-start | bytes 688136 | tf_op jit(solution)/shard_map/ppermute | solution.py:329
  13.6 11.3 %collective-permute-start = (bf16[896,128]{1,0:T(8,128)(2,1)S(1)}, bf16[896,128]{1,0:T(8,128)(2,1)S(1)}, u32[]{:S(2)}, u32[]{:S(2)}) collective-permute-start(bf16[896,128]{1,0:T(8,128)(2,1)S(1)} %get-tuple-element.54.down.refs_0_), channel_id=1, source_target_pairs={{0,248},{4,252},{8,0},{12,4},{16,8},{20,12},{24,16},{28,20},{32,24... | collective-permute-start | bytes 688136 | tf_op jit(solution)/shard_map/ppermute | solution.py:329
  18.5 9.0 %collective-permute-start.1 = (bf16[896,128]{1,0:T(8,128)(2,1)S(1)}, bf16[896,128]{1,0:T(8,128)(2,1)S(1)}, u32[]{:S(2)}, u32[]{:S(2)}) collective-permute-start(bf16[896,128]{1,0:T(8,128)(2,1)S(1)} %get-tuple-element.55.up.refs_1_), channel_id=1, source_target_pairs={{0,8},{4,12},{8,16},{12,20},{16,24},{20,28},{24,32},{28,36},{32,40... | collective-permute-start | bytes 688136 | tf_op jit(solution)/shard_map/ppermute | solution.py:329
  23.3 29.6 %collective-permute-start.11 = (bf16[2688,128]{1,0:T(8,128)(2,1)S(1)}, bf16[2688,128]{1,0:T(8,128)(2,1)S(1)}, u32[]{:S(2)}, u32[]{:S(2)}) collective-permute-start(bf16[2688,128]{1,0:T(8,128)(2,1)S(1)} %get-tuple-element.67), channel_id=1, source_target_pairs={{0,4},{4,0},{8,12},{12,8},{16,20},{20,16},{24,28},{28,24},{32,36},... | collective-permute-start | bytes 2064392 | tf_op jit(solution)/shard_map/ppermute | solution.py:329
  28.1 37.8 %collective-permute-start.5 = (bf16[2688,128]{1,0:T(8,128)(2,1)S(1)}, bf16[2688,128]{1,0:T(8,128)(2,1)S(1)}, u32[]{:S(2)}, u32[]{:S(2)}) collective-permute-start(bf16[2688,128]{1,0:T(8,128)(2,1)S(1)} %get-tuple-element.59), channel_id=1, source_target_pairs={{0,4},{4,0},{8,12},{12,8},{16,20},{20,16},{24,28},{28,24},{32,36},... | collective-permute-start | bytes 2064392 | tf_op jit(solution)/shard_map/ppermute | solution.py:329
  30.6 8.1 %collective-permute-start.8 = (bf16[640,128]{1,0:T(8,128)(2,1)S(1)}, bf16[640,128]{1,0:T(8,128)(2,1)S(1)}, u32[]{:S(2)}, u32[]{:S(2)}) collective-permute-start(bf16[640,128]{1,0:T(8,128)(2,1)S(1)} %get-tuple-element.64), channel_id=1, source_target_pairs={{0,240},{4,244},{8,248},{12,252},{16,0},{20,4},{24,8},{28,12},{32,... | collective-permute-start | bytes 491528 | tf_op jit(solution)/shard_map/ppermute | solution.py:329
  30.6 11.3 %collective-permute-start.9 = (bf16[640,128]{1,0:T(8,128)(2,1)S(1)}, bf16[640,128]{1,0:T(8,128)(2,1)S(1)}, u32[]{:S(2)}, u32[]{:S(2)}) collective-permute-start(bf16[640,128]{1,0:T(8,128)(2,1)S(1)} %get-tuple-element.65), channel_id=1, source_target_pairs={{0,16},{4,20},{8,24},{12,28},{16,32},{20,36},{24,40},{28,44},{32,4... | collective-permute-start | bytes 491528 | tf_op jit(solution)/shard_map/ppermute | solution.py:329
  38.7 14.2 %collective-permute-start.12 = (bf16[640,128]{1,0:T(8,128)(2,1)S(1)}, bf16[640,128]{1,0:T(8,128)(2,1)S(1)}, u32[]{:S(2)}, u32[]{:S(2)}) collective-permute-start(bf16[640,128]{1,0:T(8,128)(2,1)S(1)} %collective-permute-done.8.refs_4_), channel_id=1, source_target_pairs={{0,4},{4,0},{8,12},{12,8},{16,20},{20,16},{24,28},{28,24},{32,36},... | collective-permute-start | bytes 491528 | tf_op jit(solution)/shard_map/ppermute | solution.py:329
  39.7 7.2 %collective-permute-start.10 = (bf16[256,128]{1,0:T(8,128)(2,1)S(1)}, bf16[256,128]{1,0:T(8,128)(2,1)S(1)}, u32[]{:S(2)}, u32[]{:S(2)}) collective-permute-start(bf16[256,128]{1,0:T(8,128)(2,1)S(1)} %get-tuple-element.66), channel_id=1, source_target_pairs={{0,236},{4,24},{8,244},{12,32},{16,252},{20,40},{24,4},{28,48},{32... | collective-permute-start | bytes 196616 | tf_op jit(solution)/shard_map/ppermute | solution.py:329
  41.9 10.9 %collective-permute-start.13 = (bf16[640,128]{1,0:T(8,128)(2,1)S(1)}, bf16[640,128]{1,0:T(8,128)(2,1)S(1)}, u32[]{:S(2)}, u32[]{:S(2)}) collective-permute-start(bf16[640,128]{1,0:T(8,128)(2,1)S(1)} %collective-permute-done.9.refs_5_), channel_id=1, source_target_pairs={{0,4},{4,0},{8,12},{12,8},{16,20},{20,16},{24,28},{28,24},{32,36},... | collective-permute-start | bytes 491528 | tf_op jit(solution)/shard_map/ppermute | solution.py:329
  46.9 13.7 %collective-permute-start.2 = (bf16[640,128]{1,0:T(8,128)(2,1)S(1)}, bf16[640,128]{1,0:T(8,128)(2,1)S(1)}, u32[]{:S(2)}, u32[]{:S(2)}) collective-permute-start(bf16[640,128]{1,0:T(8,128)(2,1)S(1)} %get-tuple-element.56), channel_id=1, source_target_pairs={{0,240},{4,244},{8,248},{12,252},{16,0},{20,4},{24,8},{28,12},{32,... | collective-permute-start | bytes 491528 | tf_op jit(solution)/shard_map/ppermute | solution.py:329
  52.9 13.1 %collective-permute-start.3 = (bf16[640,128]{1,0:T(8,128)(2,1)S(1)}, bf16[640,128]{1,0:T(8,128)(2,1)S(1)}, u32[]{:S(2)}, u32[]{:S(2)}) collective-permute-start(bf16[640,128]{1,0:T(8,128)(2,1)S(1)} %get-tuple-element.57), channel_id=1, source_target_pairs={{0,16},{4,20},{8,24},{12,28},{16,32},{20,36},{24,40},{28,44},{32,4... | collective-permute-start | bytes 491528 | tf_op jit(solution)/shard_map/ppermute | solution.py:329
  52.9 7.7 %collective-permute-start.4 = (bf16[256,128]{1,0:T(8,128)(2,1)S(1)}, bf16[256,128]{1,0:T(8,128)(2,1)S(1)}, u32[]{:S(2)}, u32[]{:S(2)}) collective-permute-start(bf16[256,128]{1,0:T(8,128)(2,1)S(1)} %get-tuple-element.58), channel_id=1, source_target_pairs={{0,236},{4,24},{8,244},{12,32},{16,252},{20,40},{24,4},{28,48},{32... | collective-permute-start | bytes 196616 | tf_op jit(solution)/shard_map/ppermute | solution.py:329
  66.0 11.3 %collective-permute-start.14 = (bf16[896,128]{1,0:T(8,128)(2,1)S(1)}, bf16[896,128]{1,0:T(8,128)(2,1)S(1)}, u32[]{:S(2)}, u32[]{:S(2)}) collective-permute-start(bf16[896,128]{1,0:T(8,128)(2,1)S(1)} %get-tuple-element.70.down.refs_0_), channel_id=1, source_target_pairs={{0,248},{4,252},{8,0},{12,4},{16,8},{20,12},{24,16},{28,20},{32,24... | collective-permute-start | bytes 688136 | tf_op jit(solution)/shard_map/ppermute | solution.py:329
  68.8 8.7 %collective-permute-start.15 = (bf16[896,128]{1,0:T(8,128)(2,1)S(1)}, bf16[896,128]{1,0:T(8,128)(2,1)S(1)}, u32[]{:S(2)}, u32[]{:S(2)}) collective-permute-start(bf16[896,128]{1,0:T(8,128)(2,1)S(1)} %get-tuple-element.71.up.refs_1_), channel_id=1, source_target_pairs={{0,8},{4,12},{8,16},{12,20},{16,24},{20,28},{24,32},{28,36},{32,40... | collective-permute-start | bytes 688136 | tf_op jit(solution)/shard_map/ppermute | solution.py:329
  78.1 16.1 %collective-permute-start.21 = (bf16[2688,128]{1,0:T(8,128)(2,1)S(1)}, bf16[2688,128]{1,0:T(8,128)(2,1)S(1)}, u32[]{:S(2)}, u32[]{:S(2)}) collective-permute-start(bf16[2688,128]{1,0:T(8,128)(2,1)S(1)} %get-tuple-element.93), channel_id=1, source_target_pairs={{0,4},{4,0},{8,12},{12,8},{16,20},{20,16},{24,28},{28,24},{32,36},... | collective-permute-start | bytes 2064392 | tf_op jit(solution)/shard_map/ppermute | solution.py:329
  78.3 13.4 %collective-permute-start.18 = (bf16[640,128]{1,0:T(8,128)(2,1)S(1)}, bf16[640,128]{1,0:T(8,128)(2,1)S(1)}, u32[]{:S(2)}, u32[]{:S(2)}) collective-permute-start(bf16[640,128]{1,0:T(8,128)(2,1)S(1)} %get-tuple-element.90), channel_id=1, source_target_pairs={{0,240},{4,244},{8,248},{12,252},{16,0},{20,4},{24,8},{28,12},{32,... | collective-permute-start | bytes 491528 | tf_op jit(solution)/shard_map/ppermute | solution.py:329
  79.5 14.7 %collective-permute-start.19 = (bf16[640,128]{1,0:T(8,128)(2,1)S(1)}, bf16[640,128]{1,0:T(8,128)(2,1)S(1)}, u32[]{:S(2)}, u32[]{:S(2)}) collective-permute-start(bf16[640,128]{1,0:T(8,128)(2,1)S(1)} %get-tuple-element.91), channel_id=1, source_target_pairs={{0,16},{4,20},{8,24},{12,28},{16,32},{20,36},{24,40},{28,44},{32,4... | collective-permute-start | bytes 491528 | tf_op jit(solution)/shard_map/ppermute | solution.py:329
  82.3 9.4 %collective-permute-start.20 = (bf16[256,128]{1,0:T(8,128)(2,1)S(1)}, bf16[256,128]{1,0:T(8,128)(2,1)S(1)}, u32[]{:S(2)}, u32[]{:S(2)}) collective-permute-start(bf16[256,128]{1,0:T(8,128)(2,1)S(1)} %get-tuple-element.92), channel_id=1, source_target_pairs={{0,236},{4,24},{8,244},{12,32},{16,252},{20,40},{24,4},{28,48},{32... | collective-permute-start | bytes 196616 | tf_op jit(solution)/shard_map/ppermute | solution.py:329
  94.2 3.9 %collective-permute-start.22 = (f32[3456,128]{1,0:T(8,128)S(1)}, f32[3456,128]{1,0:T(8,128)S(1)}, u32[]{:S(2)}, u32[]{:S(2)}) collective-permute-start(f32[3456,128]{1,0:T(8,128)S(1)} %get-tuple-element.95), channel_id=1, source_target_pairs={{0,4},{4,0},{8,12},{12,8},{16,20},{20,16},{24,28},{28,24},{32,36},... | collective-permute-start | bytes 5308424 | tf_op jit(solution)/shard_map/ppermute | solution.py:329
  118.5 20.9 %all-to-all-start.1 = ((bf16[8,216,128]{2,1,0:T(8,128)(2,1)}), bf16[8,216,128]{2,1,0:T(8,128)(2,1)}, u32[]{:S(2)}, u32[]{:S(2)}) async-start(bf16[8,216,128]{2,1,0:T(8,128)(2,1)} %broadcast_in_dim.6), calls=%async_computation.1 | async-start | bytes 884736 | tf_op jit(solution)/shard_map/all_to_all | solution.py:373
  126.6 3.6 %collective-permute-start.23 = (bf16[640,128]{1,0:T(8,128)(2,1)S(1)}, bf16[640,128]{1,0:T(8,128)(2,1)S(1)}, u32[]{:S(2)}, u32[]{:S(2)}) collective-permute-start(bf16[640,128]{1,0:T(8,128)(2,1)S(1)} %collective-permute-done.18.refs_4_), channel_id=1, source_target_pairs={{0,4},{4,0},{8,12},{12,8},{16,20},{20,16},{24,28},{28,24},{32,36},... | collective-permute-start | bytes 491528 | tf_op jit(solution)/shard_map/ppermute | solution.py:329
  158.3 5.9 %collective-permute-start.25 = (bf16[3456,128]{1,0:T(8,128)(2,1)S(1)}, bf16[3456,128]{1,0:T(8,128)(2,1)S(1)}, u32[]{:S(2)}, u32[]{:S(2)}) collective-permute-start(bf16[3456,128]{1,0:T(8,128)(2,1)S(1)} %bitcast.34), channel_id=1, source_target_pairs={{0,4},{4,0},{8,12},{12,8},{16,20},{20,16},{24,28},{28,24},{32,36},... | collective-permute-start | bytes 2654216 | tf_op jit(solution)/shard_map/ppermute | solution.py:329
  (15 other events, 199.6 us)

commit v2 on v1

--- a/solution.py
+++ b/solution.py
@@ -1,3 +1,4 @@
+import functools
 import math
 
 import jax
@@ -26,8 +27,9 @@
 F32 = jnp.float32
 
 
-def pack_field(nb, dev, own, down, up):
-    ox, oe, oj, ol = 0, RX, RX + RE, RX + RE + RP
+def pack_field(nb, dev, own, down, up, last, f):
+    ox = f * FULL
+    oe, oj, ol = ox + RX, ox + RX + RE, ox + RX + RE + RP
 
     def body(b, carry):
         me = dev * BD + b
@@ -56,28 +58,38 @@
         return carry
 
     lax.fori_loop(0, BD, body, 0)
-
-
-def fill_tables(core, pieces, tx, te, tj, tl):
-    own_down, own_up, d1, u1, d2, u2, v4, near, wide_d, wide_u = pieces
+    first = (dev & 1) == 0
+
+    @pl.when(first)
+    def _():
+        last[f * FAR : f * FAR + FAR, :] = down[ox : ox + FAR, :]
+
+    @pl.when(jnp.logical_not(first))
+    def _():
+        last[f * FAR : f * FAR + FAR, :] = up[ox : ox + FAR, :]
+
+
+def fill_tables(core, pieces, tx, te, tj, tl, fields=1, f=0):
+    own_down, own_up, d1, u1, v4, d2, u2, near, wide_d, wide_u = pieces
     turn = 2 * core
+    full, two = f * FULL, f * (MID + FAR)
     plan = [
-        (own_down, 0, 10, 4),
-        (own_up, 0, 9, 4),
-        (d1, 0, 12, 4),
-        (u1, 0, 7, 4),
-        (d2, 0, 14, 2),
-        (u2, 0, 5, 2),
-        (d2, MID, 16, 1),
-        (u2, MID, 3, 1),
-        (v4, 0, 2 + 15 * core, 1),
-        (near, 0, 11 - 3 * core, 4),
-        (near, FULL, 13 - turn, 4),
-        (near, 2 * FULL, 8 - turn, 4),
-        (wide_d, 0, 15 - turn, 2),
-        (wide_u, 0, 6 - turn, 2),
-        (wide_d, MID, 17 - turn, 1),
-        (wide_u, MID, 4 - turn, 1),
+        (own_down, full, 10, 4),
+        (own_up, full, 9, 4),
+        (d1, full, 12, 4),
+        (u1, full, 7, 4),
+        (d2, two, 14, 2),
+        (u2, two, 5, 2),
+        (d2, two + MID, 16, 1),
+        (u2, two + MID, 3, 1),
+        (v4, f * FAR, 2 + 15 * core, 1),
+        (near, full, 11 - 3 * core, 4),
+        (near, full + fields * FULL, 13 - turn, 4),
+        (near, full + 2 * fields * FULL, 8 - turn, 4),
+        (wide_d, two, 15 - turn, 2),
+        (wide_u, two, 6 - turn, 2),
+        (wide_d, two + MID, 17 - turn, 1),
+        (wide_u, two + MID, 4 - turn, 1),
     ]
     for ref, row, slot, kind in plan:
         tx[slot] = ref[row : row + RX, :].astype(F32).reshape(BD, 64, CH)
@@ -192,14 +204,19 @@
         own[b] = ref[b].astype(F32)
 
 
-def pack_kernel(nb, dev, field, down, up, own):
+def pack_kernel(nb, dev, field, down, up, last, own):
     load_own(field, own)
-    pack_field(nb, dev[0], own, down, up)
+    pack_field(nb, dev[0], own, down, up, last, 0)
+
+
+def flip_kernel(nb, dev, weight, out):
+    for t in range(27):
+        out[t * CH : t * CH + CH, :] = weight[(26 - t) * CH : (27 - t) * CH, :].T
 
 
 def forward_kernel(nb, dev, feat, *refs):
     pieces, weight = refs[:10], refs[10]
-    hid, hid_s, pre, down, up, sh, own, tx, te, tj, tl, cf, lf, rf = refs[11:]
+    hid, hid_s, pre, down, up, last, sh, own, tx, te, tj, tl, cf, lf, rf = refs[11:]
     load_own(feat, own)
     fill_tables(dev[0] & 1, pieces, tx, te, tj, tl)
     build_shifted(nb, dev[0], own, tx, te, tj, tl, cf, lf, rf, sh)
@@ -217,7 +234,7 @@
         split_blocks(pair, first, act.astype(F32), store)
 
     conv(sh, weight, emit)
-    pack_field(nb, dev[0], own, down, up)
+    pack_field(nb, dev[0], own, down, up, last, 0)
 
 
 def backward_kernel(nb, dev, cot, *refs):
@@ -308,7 +325,7 @@
 
 
 SHIFTED = (3, 2, 10, 10, 16, CH)
-LIMIT = 36
+LIMIT = 26
 
 
 def call(kernel, outs, scratch, nb, dev, *arrays, limit=LIMIT):
@@ -333,47 +350,70 @@
     return hop(x, lambda i: 1 - 2 * (i % 2))
 
 
-def exchange_near(down, up):
-    return hop(down, lambda i: -2), hop(up, lambda i: 2)
-
-
-def forward_planes(nb, dev, down, up, d1, u1, far_down, far_up, last, near):
+def exchange_near(down, up, last):
+    d1, u1 = hop(down, lambda i: -2), hop(up, lambda i: 2)
+    if last is None:
+        return d1, u1, None
+    return d1, u1, hop(last, lambda i: -7 if i % 2 == 0 else 7)
+
+
+def forward_planes(fields, nb, dev, down, up, d1, u1, far_down, far_up, near, last):
+    full = fields * FULL
     for own, got, out in ((down, d1, far_down), (up, u1, far_up)):
-        out[0:MID, :] = own[0:MID, :]
-        out[MID : MID + FAR, :] = got[0:FAR, :]
-    near[FULL : 2 * FULL, :] = d1[...]
-    near[2 * FULL : 3 * FULL, :] = u1[...]
+        for f in range(fields):
+            at, row = f * (MID + FAR), f * FULL
+            out[at : at + MID, :] = own[row : row + MID, :]
+            out[at + MID : at + MID + FAR, :] = got[row : row + FAR, :]
+    near[full : 2 * full, :] = d1[...]
+    near[2 * full : 3 * full, :] = u1[...]
     first = (dev[0] & 1) == 0
 
     @pl.when(first)
     def _():
+        near[0:full, :] = up[...]
         last[...] = d1[0:FAR, :]
-        near[0:FULL, :] = up[...]
 
     @pl.when(jnp.logical_not(first))
     def _():
+        near[0:full, :] = down[...]
         last[...] = u1[0:FAR, :]
-        near[0:FULL, :] = down[...]
-
-
-def exchange_far(nb, dev, down, up, d1, u1):
-    outs = [((MID + FAR, CH), BF)] * 2 + [((FAR, CH), BF), ((3 * FULL, CH), BF)]
-    far_down, far_up, last, near = call(forward_planes, outs, [], nb, dev, down, up, d1, u1, limit=8)
-    v4 = hop(last, lambda i: -5 if i % 2 == 0 else 5)
+
+
+def exchange_far(nb, dev, down, up, d1, u1, fields, diagonal=False):
+    outs = [((fields * (MID + FAR), CH), BF)] * 2 + [((3 * fields * FULL, CH), BF), ((FAR, CH), BF)]
+    kernel = functools.partial(forward_planes, fields)
+    far_down, far_up, near, last = call(kernel, outs, [], nb, dev, down, up, d1, u1, limit=8)
+    v4 = hop(last, lambda i: -5 if i % 2 == 0 else 5) if diagonal else None
     d2 = hop(far_down, lambda i: -4)
     u2 = hop(far_up, lambda i: 4)
-    return d2, u2, v4, swap(near)
+    return d2, u2, swap(near), v4
 
 
 def exchange_wide(d2, u2):
     return swap(d2), swap(u2)
 
 
+def sum_kernel(scale, nb, dev, parts, out):
+    total = parts[0].astype(F32)
+    for k in range(1, parts.shape[0]):
+        total = total + parts[k].astype(F32)
+    if scale is not None:
+        total = total * scale
+    total = total.astype(BF)
+    for k in range(out.shape[0]):
+        out[k] = total
+
+
+def sum_and_spread(parts, copies, scale, nb, dev):
+    kernel = functools.partial(sum_kernel, scale)
+    return call(kernel, [((copies, *parts.shape[1:]), BF)], [], nb, dev, parts, limit=8)[0]
+
+
 def all_to_all(x, axes, groups):
     return lax.all_to_all(x, axes, 0, 0, axis_index_groups=groups, tiled=True)
 
 
-def reduce_all(keep, send, core, scale, work, given):
+def reduce_all(keep, send, core, scale, work, given, nb, dev):
     size, reps = lax.axis_size("blocks"), lax.axis_size("rep")
     length = 8
     width = size // (2 * length)
@@ -390,14 +430,11 @@
     rows = keep.shape[0] // count
     mine = keep + swap(send)
     part = all_to_all(mine.astype(BF).reshape(count, rows, CH), both, planes)
-    part = jnp.sum(part.astype(F32), axis=0).astype(BF)
+    part = sum_and_spread(part, length, None, nb, dev)
     part, given = lax.optimization_barrier((part, given))
     done = work(given)
-    part = jnp.broadcast_to(part[None], (length, rows, CH))
-    part = all_to_all(part, "blocks", columns)
-    part = (jnp.sum(part.astype(F32), axis=0) * scale).astype(BF)
+    part = sum_and_spread(all_to_all(part, "blocks", columns), count, scale, nb, dev)
     part, done = lax.optimization_barrier((part, done))
-    part = jnp.broadcast_to(part[None], (count, rows, CH))
     mine = all_to_all(part, both, planes).reshape(keep.shape)
     theirs = swap(mine)
     shape = (keep.shape[0] // CH, CH, CH)
@@ -413,24 +450,26 @@
     dev = index.astype(jnp.int32).reshape(1)
     w_one = weight_one.reshape(27 * CH, CH)
     w_two = weight_two.reshape(27 * CH, CH)
-    flipped = jnp.transpose(weight_two[::-1], (0, 2, 1)).reshape(27 * CH, CH)
-    halo = [((FULL, CH), BF)] * 2
-    f_down, f_up = call(pack_kernel, halo, scratch_own(), nb, dev, feat)
-    f_d1, f_u1 = exchange_near(f_down, f_up)
-    c_down, c_up = call(pack_kernel, halo, scratch_own(), nb, dev, cot)
-    c_d1, c_u1 = exchange_near(c_down, c_up)
-    f_d1, f_u1, flipped = lax.optimization_barrier((f_d1, f_u1, flipped))
-    f_far = exchange_far(nb, dev, f_down, f_up, f_d1, f_u1)
-    c_far = exchange_far(nb, dev, c_down, c_up, c_d1, c_u1)
-    pieces = (f_down, f_up, f_d1, f_u1, *f_far, *exchange_wide(f_far[0], f_far[1]))
-    hid, hid_s, pre, hid_down, hid_up, sh_feat = call(
+
+    def halo(fields):
+        return [((fields * FULL, CH), BF)] * 2 + [((fields * FAR, CH), BF)]
+
+    down, up, _ = call(pack_kernel, halo(1), scratch_own(), nb, dev, feat)
+    d1, u1, _ = exchange_near(down, up, None)
+    c_down, c_up, _ = call(pack_kernel, halo(1), scratch_own(), nb, dev, cot)
+    c_d1, c_u1, _ = exchange_near(c_down, c_up, None)
+    (flipped,) = call(flip_kernel, [((27 * CH, CH), BF)], [], nb, dev, w_two, limit=8)
+    d1, u1, flipped = lax.optimization_barrier((d1, u1, flipped))
+    d2, u2, near, v4 = exchange_far(nb, dev, down, up, d1, u1, 1, True)
+    c_d2, c_u2, c_near, c_v4 = exchange_far(nb, dev, c_down, c_up, c_d1, c_u1, 1, True)
+    pieces = (down, up, d1, u1, v4, d2, u2, near, *exchange_wide(d2, u2))
+    hid, hid_s, pre, hid_down, hid_up, hid_last, sh_feat = call(
         forward_kernel,
         [
             ((BD, 512, CH), BF),
             ((BD * 512, CH), BF),
             ((BD * 512, CH), F32),
-            ((FULL, CH), BF),
-            ((FULL, CH), BF),
+            *halo(1),
             (SHIFTED, BF),
         ],
         scratch_own() + scratch_build(),
@@ -440,9 +479,11 @@
         *pieces,
         w_one,
     )
-    c_far, hid_down, hid_up = lax.optimization_barrier((c_far, hid_down, hid_up))
-    d1, u1 = exchange_near(hid_down, hid_up)
-    pieces = (c_down, c_up, c_d1, c_u1, *c_far, *exchange_wide(c_far[0], c_far[1]))
+    tied = (c_d2, c_u2, c_near, c_v4), (hid_down, hid_up, hid_last)
+    (c_d2, c_u2, c_near, c_v4), (hid_down, hid_up, hid_last) = lax.optimization_barrier(tied)
+    d1, u1, v4 = exchange_near(hid_down, hid_up, hid_last)
+    c_wide = exchange_wide(c_d2, c_u2)
+    pieces = (c_down, c_up, c_d1, c_u1, c_v4, c_d2, c_u2, c_near, *c_wide)
     sh_cot, hid_t, delta_t = call(
         backward_kernel,
         [(SHIFTED, BF), ((CH, BD * 512), BF), ((CH, BD * 512), BF)],
@@ -456,7 +497,7 @@
         pre,
     )
     d1, u1, hid_t, delta_t, sh_cot = lax.optimization_barrier((d1, u1, hid_t, delta_t, sh_cot))
-    h_far = exchange_far(nb, dev, hid_down, hid_up, d1, u1)
+    h_far = exchange_far(nb, dev, hid_down, hid_up, d1, u1, 1)[:3]
     keep, send = call(
         gradient_kernel,
         [((27 * CH, CH), F32)] * 2,
@@ -468,12 +509,10 @@
         sh_feat,
         sh_cot,
     )
-    (keep, send), h_far = lax.optimization_barrier(((keep, send), h_far))
-    hid_pieces = (hid_down, hid_up, d1, u1, *h_far, *exchange_wide(h_far[0], h_far[1]))
     voxel_total = lax.axis_size("rep") * lax.axis_size("blocks") * BD * 512
     scale = 1.0 / math.sqrt(voxel_total)
 
-    def second(hid):
+    def second(far):
         return call(
             second_kernel,
             [((BD, 512, CH), BF)],
@@ -481,11 +520,17 @@
             nb,
             dev,
             hid,
-            *hid_pieces,
+            hid_down,
+            hid_up,
+            d1,
+            u1,
+            v4,
+            *far,
+            *exchange_wide(far[0], far[1]),
             w_two,
         )[0]
 
-    grad_one, grad_two, out = reduce_all(keep, send, core, scale, second, hid)
+    grad_one, grad_two, out = reduce_all(keep, send, core, scale, second, h_far, nb, dev)
     return out[None], grad_one, grad_two
 
 

time: 168 us -> 170 us (1.012)
  waiting for transfers between devices: 32.2 us -> 51.8 us
  blocking collectives: 35.7 us -> 19.8 us
  Pallas kernels: 29.5 us -> 35.1 us
  local copies, waits for them, and re-layouts: 8.65 us -> 5 us
    all_to_all x2 -> x1, blocking collectives: 35.7 us -> 19.8 us  [all_to_all(): return lax.all_to_all(x, axes, 0, 0, axis_index_groups=groups, tiled=True)]
    ppermute x26, waiting for transfers between devices: 30.5 us -> 43.3 us  [hop(): lax.ppermute(x, 'blocks', [(i, (i + shift(i)) % size) for i in range(size)])]
    all_to_all x1 -> x2, waiting for transfers between devices: 1.65 us -> 8.48 us  [all_to_all(): return lax.all_to_all(x, axes, 0, 0, axis_index_groups=groups, tiled=True)]
    pallas_call x9 -> x12, Pallas kernels: 29.5 us -> 35.1 us  [call(): pl.pallas_call(kernel, out_shape=[jax.ShapeDtypeStruct(shape, dtype) for...]
    transpose x2 -> x0, local copies, waits for them, and re-layouts: 4.12 us -> none  [slab_step(): flipped = jnp.transpose(weight_two[::-1], (0, 2, 1)).reshape(27 * CH, CH)]
    ppermute x26, starting transfers between devices: 46.7 us -> 43.8 us  [hop(): lax.ppermute(x, 'blocks', [(i, (i + shift(i)) % size) for i in range(size)])]
    reduce_sum x2 -> x0, other arithmetic: 2.37 us -> none  [the longest x1 1.29 us: reduce_all(): part = jnp.sum(part.astype(F32), axis=0).astype(BF)]
    all_to_all x1 -> x2, starting transfers between devices: 8.04 us -> 9.39 us  [all_to_all(): return lax.all_to_all(x, axes, 0, 0, axis_index_groups=groups, tiled=True)]
  transfers between devices with their start and end apart: 27 -> 28, of which waited for: 15 -> 13; matrix products, arithmetic and copies ran while one was open for 2% -> 0% of each run, Pallas kernels for 17% -> 16%
where the time goes in v2:
time: 170 us
  starting transfers between devices  53.2 us (31%)
  waiting for transfers between devices  51.8 us (30%)
  Pallas kernels  35.1 us (21%)
  blocking collectives  19.8 us (12%)
  local copies, waits for them, and re-layouts  5 us (3%)
  other arithmetic  4.17 us (2%)
    ppermute x26, starting transfers between devices, hop(): lax.ppermute(x, 'blocks', [(i, (i + shift(i)) % size) for i in range(size)])  43.8 us
    ppermute x26, waiting for transfers between devices, hop(): lax.ppermute(x, 'blocks', [(i, (i + shift(i)) % size) for i in range(size)])  43.3 us
    pallas_call x12, Pallas kernels, call(): pl.pallas_call(kernel, out_shape=[jax.ShapeDtypeStruct(shape, dtype) for...  35.1 us
    all_to_all x1, blocking collectives, all_to_all(): return lax.all_to_all(x, axes, 0, 0, axis_index_groups=groups, tiled=True)  19.8 us
    all_to_all x2, starting transfers between devices, all_to_all(): return lax.all_to_all(x, axes, 0, 0, axis_index_groups=groups, tiled=True)  9.39 us
    all_to_all x2, waiting for transfers between devices, all_to_all(): return lax.all_to_all(x, axes, 0, 0, axis_index_groups=groups, tiled=True)  8.48 us
    unnamed x24, local copies, waits for them, and re-layouts  5 us
  transfers between devices with their start and end apart: 28, of which 13 were waited for; matrix products, arithmetic and copies ran while one was open for 0% of the time, Pallas kernels for 16%

profile of v2, /device:TPU:1, one launch (start us, length us, event | category | flops | bytes accessed | tf_op | source)
XLA Modules:
  0.0 169.9 jit_solution(13366268737344094576)
XLA Ops:
  3.8 8.6 %collective-permute-start.6 = (bf16[896,128]{1,0:T(8,128)(2,1)S(1)}, bf16[896,128]{1,0:T(8,128)(2,1)S(1)}, u32[]{:S(2)}, u32[]{:S(2)}) collective-permute-start(bf16[896,128]{1,0:T(8,128)(2,1)S(1)} %get-tuple-element.57.down.refs_0_), channel_id=1, source_target_pairs={{0,248},{4,252},{8,0},{12,4},{16,8},{20,12},{24,16},{28,20},{32,24... | collective-permute-start | bytes 688136 | tf_op jit(solution)/shard_map/ppermute | solution.py:346
  14.8 4.8 %collective-permute-start = (bf16[896,128]{1,0:T(8,128)(2,1)S(1)}, bf16[896,128]{1,0:T(8,128)(2,1)S(1)}, u32[]{:S(2)}, u32[]{:S(2)}) collective-permute-start(bf16[896,128]{1,0:T(8,128)(2,1)S(1)} %get-tuple-element.51.down.refs_0_), channel_id=1, source_target_pairs={{0,248},{4,252},{8,0},{12,4},{16,8},{20,12},{24,16},{28,20},{32,24... | collective-permute-start | bytes 688136 | tf_op jit(solution)/shard_map/ppermute | solution.py:346
  24.5 4.1 %collective-permute-done.1.u1.refs_3_ = bf16[896,128]{1,0:T(8,128)(2,1)S(1)} collective-permute-done((bf16[896,128]{1,0:T(8,128)(2,1)S(1)}, bf16[896,128]{1,0:T(8,128)(2,1)S(1)}, u32[]{:S(2)}, u32[]{:S(2)}) %collective-permute-start.1) | collective-permute-done | bytes 229408 | tf_op jit(solution)/shard_map/ppermute | solution.py:346
  29.2 2.5 %collective-permute-start.4 = (bf16[2688,128]{1,0:T(8,128)(2,1)S(1)}, bf16[2688,128]{1,0:T(8,128)(2,1)S(1)}, u32[]{:S(2)}, u32[]{:S(2)}) collective-permute-start(bf16[2688,128]{1,0:T(8,128)(2,1)S(1)} %get-tuple-element.55), channel_id=1, source_target_pairs={{0,4},{4,0},{8,12},{12,8},{16,20},{20,16},{24,28},{28,24},{32,36},... | collective-permute-start | bytes 2064392 | tf_op jit(solution)/shard_map/ppermute | solution.py:346
  31.7 2.4 %collective-permute-start.10 = (bf16[640,128]{1,0:T(8,128)(2,1)S(1)}, bf16[640,128]{1,0:T(8,128)(2,1)S(1)}, u32[]{:S(2)}, u32[]{:S(2)}) collective-permute-start(bf16[640,128]{1,0:T(8,128)(2,1)S(1)} %get-tuple-element.63), channel_id=1, source_target_pairs={{0,16},{4,20},{8,24},{12,28},{16,32},{20,36},{24,40},{28,44},{32,4... | collective-permute-start | bytes 491528 | tf_op jit(solution)/shard_map/ppermute | solution.py:346
  34.1 5.8 %collective-permute-done.9.refs_5_ = bf16[640,128]{1,0:T(8,128)(2,1)S(1)} collective-permute-done((bf16[640,128]{1,0:T(8,128)(2,1)S(1)}, bf16[640,128]{1,0:T(8,128)(2,1)S(1)}, u32[]{:S(2)}, u32[]{:S(2)}) %collective-permute-start.9) | collective-permute-done | bytes 163872 | tf_op jit(solution)/shard_map/ppermute | solution.py:346
  44.1 4.0 %collective-permute-done.8.refs_4_ = bf16[256,128]{1,0:T(8,128)(2,1)S(1)} collective-permute-done((bf16[256,128]{1,0:T(8,128)(2,1)S(1)}, bf16[256,128]{1,0:T(8,128)(2,1)S(1)}, u32[]{:S(2)}, u32[]{:S(2)}) %collective-permute-start.8) | collective-permute-done | bytes 65568 | tf_op jit(solution)/shard_map/ppermute | solution.py:346
  48.1 6.2 %collective-permute-start.2 = (bf16[640,128]{1,0:T(8,128)(2,1)S(1)}, bf16[640,128]{1,0:T(8,128)(2,1)S(1)}, u32[]{:S(2)}, u32[]{:S(2)}) collective-permute-start(bf16[640,128]{1,0:T(8,128)(2,1)S(1)} %get-tuple-element.53), channel_id=1, source_target_pairs={{0,240},{4,244},{8,248},{12,252},{16,0},{20,4},{24,8},{28,12},{32,... | collective-permute-start | bytes 491528 | tf_op jit(solution)/shard_map/ppermute | solution.py:346
  54.4 6.7 %shard_map.81 = (bf16[4,512,128]{2,1,0:T(8,128)(2,1)S(1)}, bf16[2048,128]{1,0:T(8,128)(2,1)S(1)}, f32[2048,128]{1,0:T(8,128)S(1)}, bf16[896,128]{1,0:T(8,128)(2,...) custom-call(s32[4,26]{1,0:T(4,128)S(1)} %bitcast.27, ...), custom_call_target="tpu_custom_call" | custom-call | tf_op jit(solution)/shard_map/pallas_call | solution.py:334
  61.2 6.2 %collective-permute-done.3.refs_6_ = bf16[640,128]{1,0:T(8,128)(2,1)S(1)} collective-permute-done((bf16[640,128]{1,0:T(8,128)(2,1)S(1)}, bf16[640,128]{1,0:T(8,128)(2,1)S(1)}, u32[]{:S(2)}, u32[]{:S(2)}) %collective-permute-start.3) | collective-permute-done | bytes 163872 | tf_op jit(solution)/shard_map/ppermute | solution.py:346
  67.4 2.3 %collective-permute-start.14 = (bf16[896,128]{1,0:T(8,128)(2,1)S(1)}, bf16[896,128]{1,0:T(8,128)(2,1)S(1)}, u32[]{:S(2)}, u32[]{:S(2)}) collective-permute-start(bf16[896,128]{1,0:T(8,128)(2,1)S(1)} %get-tuple-element.68.down.refs_0_), channel_id=1, source_target_pairs={{0,248},{4,252},{8,0},{12,4},{16,8},{20,12},{24,16},{28,20},{32,24... | collective-permute-start | bytes 688136 | tf_op jit(solution)/shard_map/ppermute | solution.py:346
  72.1 6.8 %shard_map.82 = (bf16[3,2,10,10,16,128]{5,4,3,2,1,0:T(8,128)(2,1)S(1)}, bf16[128,2048]{1,0:T(8,128)(2,1)S(1)}, bf16[128,2048]{1,0:T(8,128)(2,1)S(1)}) custom-call(s32[4,26]{1,0:T(4,128)S(1)} %bitcast.28, s32[1]{0:T(128)} %bitcast.1.dev, bf16[4,512,128]{2,1,0:T(8,128)(2,1)S(1)} %bitcast.20, bf16[896,128]{1,0:T(8,128)(2,1)S(1)} %get-tuple-element.51.down.refs_0_, ...), custom_call_target="tpu_custom_call" | custom-call | tf_op jit(solution)/shard_map/pallas_call | solution.py:334
  78.9 5.3 %shard_map.83 = (f32[3456,128]{1,0:T(8,128)S(1)}, f32[3456,128]{1,0:T(8,128)S(1)}) custom-call(s32[4,26]{1,0:T(4,128)S(1)} %bitcast.29, s32[1]{0:T(128)} %bitcast.1.dev, bf16[128,2048]{1,0:T(8,128)(2,1)S(1)} %get-tuple-element.80.hid_t, bf16[128,2048]{1,0:T(8,128)(2,1)S(1)} %get-tuple-element.81.delta_t, ...), custom_call_target="tpu_custom_call" | custom-call | tf_op jit(solution)/shard_map/pallas_call | solution.py:334
  84.6 3.5 %collective-permute-done.18 = f32[3456,128]{1,0:T(8,128)S(1)} collective-permute-done((f32[3456,128]{1,0:T(8,128)S(1)}, f32[3456,128]{1,0:T(8,128)S(1)}, u32[]{:S(2)}, u32[]{:S(2)}) %collective-permute-start.18) | collective-permute-done | bytes 1769504 | tf_op jit(solution)/shard_map/ppermute | solution.py:346
  89.2 4.4 %all-to-all-start = ((bf16[16,216,128]{2,1,0:T(8,128)(2,1)}), bf16[16,216,128]{2,1,0:T(8,128)(2,1)S(1)}, u32[]{:S(2)}, u32[]{:S(2)}) async-start(bf16[16,216,128]{2,1,0:T(8,128)(2,1)} %bitcast.6), calls=%async_computation | async-start | bytes 1769472 | tf_op jit(solution)/shard_map/all_to_all | solution.py:413
  95.8 3.1 %collective-permute-start.19 = (bf16[640,128]{1,0:T(8,128)(2,1)}, bf16[640,128]{1,0:T(8,128)(2,1)S(1)}, u32[]{:S(2)}, u32[]{:S(2)}) collective-permute-start(bf16[640,128]{1,0:T(8,128)(2,1)} %get-tuple-element.88), channel_id=1, source_target_pairs={{0,240},{4,244},{8,248},{12,252},{16,0},{20,4},{24,8},{28,12},{32,... | collective-permute-start | bytes 491528 | tf_op jit(solution)/shard_map/ppermute | solution.py:346
  99.0 8.5 %all-to-all-done.parts = bf16[16,216,128]{2,1,0:T(8,128)(2,1)S(1)} async-done(((bf16[16,216,128]{2,1,0:T(8,128)(2,1)}), bf16[16,216,128]{2,1,0:T(8,128)(2,1)S(1)}, u32[]{:S(2)}, u32[]{:S(2)}) %all-to-all-start) | async-done | bytes 884768 | tf_op jit(solution)/shard_map/all_to_all | solution.py:413
  109.0 2.6 %collective-permute-done.20.refs_6_ = bf16[640,128]{1,0:T(8,128)(2,1)} collective-permute-done((bf16[640,128]{1,0:T(8,128)(2,1)}, bf16[640,128]{1,0:T(8,128)(2,1)}, u32[]{:S(2)}, u32[]{:S(2)}) %collective-permute-start.20) | collective-permute-done | bytes 163872 | tf_op jit(solution)/shard_map/ppermute | solution.py:346
  111.6 5.0 %all-to-all-start.1 = ((bf16[8,216,128]{2,1,0:T(8,128)(2,1)}), bf16[8,216,128]{2,1,0:T(8,128)(2,1)S(1)}, u32[]{:S(2)}, u32[]{:S(2)}) async-start(bf16[8,216,128]{2,1,0:T(8,128)(2,1)} %shard_map.84), calls=%async_computation.1 | async-start | bytes 884736 | tf_op jit(solution)/shard_map/all_to_all | solution.py:413
  118.5 6.0 %collective-permute-start.22 = (bf16[256,128]{1,0:T(8,128)(2,1)}, bf16[256,128]{1,0:T(8,128)(2,1)S(1)}, u32[]{:S(2)}, u32[]{:S(2)}) collective-permute-start(bf16[256,128]{1,0:T(8,128)(2,1)} %copy-done.11), channel_id=1, source_target_pairs={{0,228},{4,32},{8,236},{12,40},{16,244},{20,48},{24,252},{28,56},{... | collective-permute-start | bytes 196616 | tf_op jit(solution)/shard_map/ppermute | solution.py:346
  124.5 10.9 %collective-permute-done.22.refs_4_ = bf16[256,128]{1,0:T(8,128)(2,1)S(1)} collective-permute-done((bf16[256,128]{1,0:T(8,128)(2,1)}, bf16[256,128]{1,0:T(8,128)(2,1)S(1)}, u32[]{:S(2)}, u32[]{:S(2)}) %collective-permute-start.22) | collective-permute-done | bytes 65568 | tf_op jit(solution)/shard_map/ppermute | solution.py:346
  136.4 7.6 %shard_map.87 = bf16[4,512,128]{2,1,0:T(8,128)(2,1)} custom-call(s32[4,26]{1,0:T(4,128)S(1)} %bitcast.32, s32[1]{0:T(128)} %bitcast.1.dev, bf16[4,512,128]{2,1,0:T(8,128)(2,1)S(1)} %copy-done.8, bf16[896,128]{1,0:T(8,128)(2,1)S(1)} %get-tuple-element.68.down.refs_0_, bf16[896,128]{1,0:T(8,128)(2,1)S(1)} %get-tuple-element.69.up.refs_1_, ...), custom_call_target="tpu_custom_call" | custom-call | tf_op jit(solution)/shard_map/pallas_call | solution.py:334
  144.7 19.8 %all_to_all.15 = bf16[16,216,128]{2,1,0:T(8,128)(2,1)S(1)} all-to-all(bf16[16,216,128]{2,1,0:T(8,128)(2,1)S(1)} %shard_map.86), channel_id=1, replica_groups={{0,1,2,3,64,65,66,67,128,129,130,131,192,193,194,195},{4,5,6,7,68,69,70..., dimensions={0} | all-to-all | bytes 1769472 | tf_op jit(solution)/shard_map/all_to_all | solution.py:413
  164.5 2.4 %collective-permute-done.25 = bf16[3456,128]{1,0:T(8,128)(2,1)S(1)} collective-permute-done((bf16[3456,128]{1,0:T(8,128)(2,1)S(1)}, bf16[3456,128]{1,0:T(8,128)(2,1)S(1)}, u32[]{:S(2)}, u32[]{:S(2)}) %collective-permute-start.25) | collective-permute-done | bytes 884768 | tf_op jit(solution)/shard_map/ppermute | solution.py:346
  (73 shorter events, 29.8 us)
Async XLA Ops:
  3.8 17.9 %collective-permute-start.6 = (bf16[896,128]{1,0:T(8,128)(2,1)S(1)}, bf16[896,128]{1,0:T(8,128)(2,1)S(1)}, u32[]{:S(2)}, u32[]{:S(2)}) collective-permute-start(bf16[896,128]{1,0:T(8,128)(2,1)S(1)} %get-tuple-element.57.down.refs_0_), channel_id=1, source_target_pairs={{0,248},{4,252},{8,0},{12,4},{16,8},{20,12},{24,16},{28,20},{32,24... | collective-permute-start | bytes 688136 | tf_op jit(solution)/shard_map/ppermute | solution.py:346
  12.4 9.5 %collective-permute-start.7 = (bf16[896,128]{1,0:T(8,128)(2,1)S(1)}, bf16[896,128]{1,0:T(8,128)(2,1)S(1)}, u32[]{:S(2)}, u32[]{:S(2)}) collective-permute-start(bf16[896,128]{1,0:T(8,128)(2,1)S(1)} %get-tuple-element.58.up.refs_1_), channel_id=1, source_target_pairs={{0,8},{4,12},{8,16},{12,20},{16,24},{20,28},{24,32},{28,36},{32,40... | collective-permute-start | bytes 688136 | tf_op jit(solution)/shard_map/ppermute | solution.py:346
  14.8 9.6 %collective-permute-start = (bf16[896,128]{1,0:T(8,128)(2,1)S(1)}, bf16[896,128]{1,0:T(8,128)(2,1)S(1)}, u32[]{:S(2)}, u32[]{:S(2)}) collective-permute-start(bf16[896,128]{1,0:T(8,128)(2,1)S(1)} %get-tuple-element.51.down.refs_0_), channel_id=1, source_target_pairs={{0,248},{4,252},{8,0},{12,4},{16,8},{20,12},{24,16},{28,20},{32,24... | collective-permute-start | bytes 688136 | tf_op jit(solution)/shard_map/ppermute | solution.py:346
  19.6 9.0 %collective-permute-start.1 = (bf16[896,128]{1,0:T(8,128)(2,1)S(1)}, bf16[896,128]{1,0:T(8,128)(2,1)S(1)}, u32[]{:S(2)}, u32[]{:S(2)}) collective-permute-start(bf16[896,128]{1,0:T(8,128)(2,1)S(1)} %get-tuple-element.52.up.refs_1_), channel_id=1, source_target_pairs={{0,8},{4,12},{8,16},{12,20},{16,24},{20,28},{24,32},{28,36},{32,40... | collective-permute-start | bytes 688136 | tf_op jit(solution)/shard_map/ppermute | solution.py:346
  22.6 31.8 %collective-permute-start.11 = (bf16[2688,128]{1,0:T(8,128)(2,1)S(1)}, bf16[2688,128]{1,0:T(8,128)(2,1)S(1)}, u32[]{:S(2)}, u32[]{:S(2)}) collective-permute-start(bf16[2688,128]{1,0:T(8,128)(2,1)S(1)} %get-tuple-element.64), channel_id=1, source_target_pairs={{0,4},{4,0},{8,12},{12,8},{16,20},{20,16},{24,28},{28,24},{32,36},... | collective-permute-start | bytes 2064392 | tf_op jit(solution)/shard_map/ppermute | solution.py:346
  29.2 38.2 %collective-permute-start.4 = (bf16[2688,128]{1,0:T(8,128)(2,1)S(1)}, bf16[2688,128]{1,0:T(8,128)(2,1)S(1)}, u32[]{:S(2)}, u32[]{:S(2)}) collective-permute-start(bf16[2688,128]{1,0:T(8,128)(2,1)S(1)} %get-tuple-element.55), channel_id=1, source_target_pairs={{0,4},{4,0},{8,12},{12,8},{16,20},{20,16},{24,28},{28,24},{32,36},... | collective-permute-start | bytes 2064392 | tf_op jit(solution)/shard_map/ppermute | solution.py:346
  31.7 8.2 %collective-permute-start.9 = (bf16[640,128]{1,0:T(8,128)(2,1)S(1)}, bf16[640,128]{1,0:T(8,128)(2,1)S(1)}, u32[]{:S(2)}, u32[]{:S(2)}) collective-permute-start(bf16[640,128]{1,0:T(8,128)(2,1)S(1)} %get-tuple-element.62), channel_id=1, source_target_pairs={{0,240},{4,244},{8,248},{12,252},{16,0},{20,4},{24,8},{28,12},{32,... | collective-permute-start | bytes 491528 | tf_op jit(solution)/shard_map/ppermute | solution.py:346
  31.7 11.3 %collective-permute-start.10 = (bf16[640,128]{1,0:T(8,128)(2,1)S(1)}, bf16[640,128]{1,0:T(8,128)(2,1)S(1)}, u32[]{:S(2)}, u32[]{:S(2)}) collective-permute-start(bf16[640,128]{1,0:T(8,128)(2,1)S(1)} %get-tuple-element.63), channel_id=1, source_target_pairs={{0,16},{4,20},{8,24},{12,28},{16,32},{20,36},{24,40},{28,44},{32,4... | collective-permute-start | bytes 491528 | tf_op jit(solution)/shard_map/ppermute | solution.py:346
  39.9 14.4 %collective-permute-start.12 = (bf16[640,128]{1,0:T(8,128)(2,1)S(1)}, bf16[640,128]{1,0:T(8,128)(2,1)S(1)}, u32[]{:S(2)}, u32[]{:S(2)}) collective-permute-start(bf16[640,128]{1,0:T(8,128)(2,1)S(1)} %collective-permute-done.9.refs_5_), channel_id=1, source_target_pairs={{0,4},{4,0},{8,12},{12,8},{16,20},{20,16},{24,28},{28,24},{32,36},... | collective-permute-start | bytes 491528 | tf_op jit(solution)/shard_map/ppermute | solution.py:346
  40.9 7.2 %collective-permute-start.8 = (bf16[256,128]{1,0:T(8,128)(2,1)S(1)}, bf16[256,128]{1,0:T(8,128)(2,1)S(1)}, u32[]{:S(2)}, u32[]{:S(2)}) collective-permute-start(bf16[256,128]{1,0:T(8,128)(2,1)S(1)} %get-tuple-element.61), channel_id=1, source_target_pairs={{0,236},{4,24},{8,244},{12,32},{16,252},{20,40},{24,4},{28,48},{32... | collective-permute-start | bytes 196616 | tf_op jit(solution)/shard_map/ppermute | solution.py:346
  43.0 11.3 %collective-permute-start.13 = (bf16[640,128]{1,0:T(8,128)(2,1)S(1)}, bf16[640,128]{1,0:T(8,128)(2,1)S(1)}, u32[]{:S(2)}, u32[]{:S(2)}) collective-permute-start(bf16[640,128]{1,0:T(8,128)(2,1)S(1)} %collective-permute-done.10.refs_6_), channel_id=1, source_target_pairs={{0,4},{4,0},{8,12},{12,8},{16,20},{20,16},{24,28},{28,24},{32,36},... | collective-permute-start | bytes 491528 | tf_op jit(solution)/shard_map/ppermute | solution.py:346
  48.1 13.1 %collective-permute-start.2 = (bf16[640,128]{1,0:T(8,128)(2,1)S(1)}, bf16[640,128]{1,0:T(8,128)(2,1)S(1)}, u32[]{:S(2)}, u32[]{:S(2)}) collective-permute-start(bf16[640,128]{1,0:T(8,128)(2,1)S(1)} %get-tuple-element.53), channel_id=1, source_target_pairs={{0,240},{4,244},{8,248},{12,252},{16,0},{20,4},{24,8},{28,12},{32,... | collective-permute-start | bytes 491528 | tf_op jit(solution)/shard_map/ppermute | solution.py:346
  54.3 13.1 %collective-permute-start.3 = (bf16[640,128]{1,0:T(8,128)(2,1)S(1)}, bf16[640,128]{1,0:T(8,128)(2,1)S(1)}, u32[]{:S(2)}, u32[]{:S(2)}) collective-permute-start(bf16[640,128]{1,0:T(8,128)(2,1)S(1)} %get-tuple-element.54), channel_id=1, source_target_pairs={{0,16},{4,20},{8,24},{12,28},{16,32},{20,36},{24,40},{28,44},{32,4... | collective-permute-start | bytes 491528 | tf_op jit(solution)/shard_map/ppermute | solution.py:346
  54.3 6.9 %collective-permute-start.5 = (bf16[256,128]{1,0:T(8,128)(2,1)S(1)}, bf16[256,128]{1,0:T(8,128)(2,1)S(1)}, u32[]{:S(2)}, u32[]{:S(2)}) collective-permute-start(bf16[256,128]{1,0:T(8,128)(2,1)S(1)} %get-tuple-element.56), channel_id=1, source_target_pairs={{0,236},{4,24},{8,244},{12,32},{16,252},{20,40},{24,4},{28,48},{32... | collective-permute-start | bytes 196616 | tf_op jit(solution)/shard_map/ppermute | solution.py:346
  67.4 11.5 %collective-permute-start.14 = (bf16[896,128]{1,0:T(8,128)(2,1)S(1)}, bf16[896,128]{1,0:T(8,128)(2,1)S(1)}, u32[]{:S(2)}, u32[]{:S(2)}) collective-permute-start(bf16[896,128]{1,0:T(8,128)(2,1)S(1)} %get-tuple-element.68.down.refs_0_), channel_id=1, source_target_pairs={{0,248},{4,252},{8,0},{12,4},{16,8},{20,12},{24,16},{28,20},{32,24... | collective-permute-start | bytes 688136 | tf_op jit(solution)/shard_map/ppermute | solution.py:346
  69.7 9.3 %collective-permute-start.15 = (bf16[896,128]{1,0:T(8,128)(2,1)S(1)}, bf16[896,128]{1,0:T(8,128)(2,1)S(1)}, u32[]{:S(2)}, u32[]{:S(2)}) collective-permute-start(bf16[896,128]{1,0:T(8,128)(2,1)S(1)} %get-tuple-element.69.up.refs_1_), channel_id=1, source_target_pairs={{0,8},{4,12},{8,16},{12,20},{16,24},{20,28},{24,32},{28,36},{32,40... | collective-permute-start | bytes 688136 | tf_op jit(solution)/shard_map/ppermute | solution.py:346
  89.2 18.3 %all-to-all-start = ((bf16[16,216,128]{2,1,0:T(8,128)(2,1)}), bf16[16,216,128]{2,1,0:T(8,128)(2,1)S(1)}, u32[]{:S(2)}, u32[]{:S(2)}) async-start(bf16[16,216,128]{2,1,0:T(8,128)(2,1)} %bitcast.6), calls=%async_computation | async-start | bytes 1769472 | tf_op jit(solution)/shard_map/all_to_all | solution.py:413
  95.3 16.3 %collective-permute-start.21 = (bf16[2688,128]{1,0:T(8,128)(2,1)}, bf16[2688,128]{1,0:T(8,128)(2,1)S(1)}, u32[]{:S(2)}, u32[]{:S(2)}) collective-permute-start(bf16[2688,128]{1,0:T(8,128)(2,1)} %get-tuple-element.90), channel_id=1, source_target_pairs={{0,4},{4,0},{8,12},{12,8},{16,20},{20,16},{24,28},{28,24},{32,36},... | collective-permute-start | bytes 2064392 | tf_op jit(solution)/shard_map/ppermute | solution.py:346
  95.8 13.2 %collective-permute-start.19 = (bf16[640,128]{1,0:T(8,128)(2,1)}, bf16[640,128]{1,0:T(8,128)(2,1)S(1)}, u32[]{:S(2)}, u32[]{:S(2)}) collective-permute-start(bf16[640,128]{1,0:T(8,128)(2,1)} %get-tuple-element.88), channel_id=1, source_target_pairs={{0,240},{4,244},{8,248},{12,252},{16,0},{20,4},{24,8},{28,12},{32,... | collective-permute-start | bytes 491528 | tf_op jit(solution)/shard_map/ppermute | solution.py:346
  98.9 12.7 %collective-permute-start.20 = (bf16[640,128]{1,0:T(8,128)(2,1)}, bf16[640,128]{1,0:T(8,128)(2,1)}, u32[]{:S(2)}, u32[]{:S(2)}) collective-permute-start(bf16[640,128]{1,0:T(8,128)(2,1)} %get-tuple-element.89), channel_id=1, source_target_pairs={{0,16},{4,20},{8,24},{12,28},{16,32},{20,36},{24,40},{28,44},{32,4... | collective-permute-start | bytes 491528 | tf_op jit(solution)/shard_map/ppermute | solution.py:346
  111.6 32.4 %all-to-all-start.1 = ((bf16[8,216,128]{2,1,0:T(8,128)(2,1)}), bf16[8,216,128]{2,1,0:T(8,128)(2,1)S(1)}, u32[]{:S(2)}, u32[]{:S(2)}) async-start(bf16[8,216,128]{2,1,0:T(8,128)(2,1)} %shard_map.84), calls=%async_computation.1 | async-start | bytes 884736 | tf_op jit(solution)/shard_map/all_to_all | solution.py:413
  116.5 18.8 %collective-permute-start.23 = (bf16[640,128]{1,0:T(8,128)(2,1)S(1)}, bf16[640,128]{1,0:T(8,128)(2,1)S(1)}, u32[]{:S(2)}, u32[]{:S(2)}) collective-permute-start(bf16[640,128]{1,0:T(8,128)(2,1)S(1)} %collective-permute-done.19.refs_5_), channel_id=1, source_target_pairs={{0,4},{4,0},{8,12},{12,8},{16,20},{20,16},{24,28},{28,24},{32,36},... | collective-permute-start | bytes 491528 | tf_op jit(solution)/shard_map/ppermute | solution.py:346
  118.4 17.0 %collective-permute-start.24 = (bf16[640,128]{1,0:T(8,128)(2,1)}, bf16[640,128]{1,0:T(8,128)(2,1)S(1)}, u32[]{:S(2)}, u32[]{:S(2)}) collective-permute-start(bf16[640,128]{1,0:T(8,128)(2,1)} %collective-permute-done.20.refs_6_), channel_id=1, source_target_pairs={{0,4},{4,0},{8,12},{12,8},{16,20},{20,16},{24,28},{28,24},{32,36},... | collective-permute-start | bytes 491528 | tf_op jit(solution)/shard_map/ppermute | solution.py:346
  118.5 16.9 %collective-permute-start.22 = (bf16[256,128]{1,0:T(8,128)(2,1)}, bf16[256,128]{1,0:T(8,128)(2,1)S(1)}, u32[]{:S(2)}, u32[]{:S(2)}) collective-permute-start(bf16[256,128]{1,0:T(8,128)(2,1)} %copy-done.11), channel_id=1, source_target_pairs={{0,228},{4,32},{8,236},{12,40},{16,244},{20,48},{24,252},{28,56},{... | collective-permute-start | bytes 196616 | tf_op jit(solution)/shard_map/ppermute | solution.py:346
  (16 other events, 181.3 us)

commit v3 on v2

--- a/solution.py
+++ b/solution.py
@@ -58,6 +58,8 @@
         return carry
 
     lax.fori_loop(0, BD, body, 0)
+    if last is None:
+        return
     first = (dev & 1) == 0
 
     @pl.when(first)
@@ -204,9 +206,9 @@
         own[b] = ref[b].astype(F32)
 
 
-def pack_kernel(nb, dev, field, down, up, last, own):
+def pack_kernel(nb, dev, field, down, up, own):
     load_own(field, own)
-    pack_field(nb, dev[0], own, down, up, last, 0)
+    pack_field(nb, dev[0], own, down, up, None, 0)
 
 
 def flip_kernel(nb, dev, weight, out):
@@ -357,7 +359,7 @@
     return d1, u1, hop(last, lambda i: -7 if i % 2 == 0 else 7)
 
 
-def forward_planes(fields, nb, dev, down, up, d1, u1, far_down, far_up, near, last):
+def forward_planes(fields, nb, dev, down, up, d1, u1, far_down, far_up, near, *last):
     full = fields * FULL
     for own, got, out in ((down, d1, far_down), (up, u1, far_up)):
         for f in range(fields):
@@ -371,19 +373,22 @@
     @pl.when(first)
     def _():
         near[0:full, :] = up[...]
-        last[...] = d1[0:FAR, :]
+        for ref in last:
+            ref[...] = d1[0:FAR, :]
 
     @pl.when(jnp.logical_not(first))
     def _():
         near[0:full, :] = down[...]
-        last[...] = u1[0:FAR, :]
+        for ref in last:
+            ref[...] = u1[0:FAR, :]
 
 
 def exchange_far(nb, dev, down, up, d1, u1, fields, diagonal=False):
-    outs = [((fields * (MID + FAR), CH), BF)] * 2 + [((3 * fields * FULL, CH), BF), ((FAR, CH), BF)]
+    outs = [((fields * (MID + FAR), CH), BF)] * 2 + [((3 * fields * FULL, CH), BF)]
+    outs += [((FAR, CH), BF)] * diagonal
     kernel = functools.partial(forward_planes, fields)
-    far_down, far_up, near, last = call(kernel, outs, [], nb, dev, down, up, d1, u1, limit=8)
-    v4 = hop(last, lambda i: -5 if i % 2 == 0 else 5) if diagonal else None
+    far_down, far_up, near, *last = call(kernel, outs, [], nb, dev, down, up, d1, u1, limit=8)
+    v4 = hop(last[0], lambda i: -5 if i % 2 == 0 else 5) if diagonal else None
     d2 = hop(far_down, lambda i: -4)
     u2 = hop(far_up, lambda i: 4)
     return d2, u2, swap(near), v4
@@ -429,7 +434,9 @@
     count = width * reps
     rows = keep.shape[0] // count
     mine = keep + swap(send)
-    part = all_to_all(mine.astype(BF).reshape(count, rows, CH), both, planes)
+    mine, given = lax.optimization_barrier((mine.astype(BF), given))
+    given = (*given, *exchange_wide(given[0], given[1]))
+    part = all_to_all(mine.reshape(count, rows, CH), both, planes)
     part = sum_and_spread(part, length, None, nb, dev)
     part, given = lax.optimization_barrier((part, given))
     done = work(given)
@@ -454,9 +461,9 @@
     def halo(fields):
         return [((fields * FULL, CH), BF)] * 2 + [((fields * FAR, CH), BF)]
 
-    down, up, _ = call(pack_kernel, halo(1), scratch_own(), nb, dev, feat)
+    down, up = call(pack_kernel, halo(1)[:2], scratch_own(), nb, dev, feat)
     d1, u1, _ = exchange_near(down, up, None)
-    c_down, c_up, _ = call(pack_kernel, halo(1), scratch_own(), nb, dev, cot)
+    c_down, c_up = call(pack_kernel, halo(1)[:2], scratch_own(), nb, dev, cot)
     c_d1, c_u1, _ = exchange_near(c_down, c_up, None)
     (flipped,) = call(flip_kernel, [((27 * CH, CH), BF)], [], nb, dev, w_two, limit=8)
     d1, u1, flipped = lax.optimization_barrier((d1, u1, flipped))
@@ -526,7 +533,6 @@
             u1,
             v4,
             *far,
-            *exchange_wide(far[0], far[1]),
             w_two,
         )[0]
 

time: 170 us -> 178 us (1.047)
  waiting for transfers between devices: 51.8 us -> 57.6 us
  starting transfers between devices: 53.2 us -> 56.6 us
  Pallas kernels: 35.1 us -> 32.9 us
  local copies, waits for them, and re-layouts: 5 us -> 7.19 us
  blocking collectives: 19.8 us -> 18 us
    all_to_all x2, waiting for transfers between devices: 8.48 us -> 12.8 us  [all_to_all(): return lax.all_to_all(x, axes, 0, 0, axis_index_groups=groups, tiled=True)]
    ppermute x26, starting transfers between devices: 43.8 us -> 46.4 us  [hop(): lax.ppermute(x, 'blocks', [(i, (i + shift(i)) % size) for i in range(size)])]
    unnamed x24 -> x28, local copies, waits for them, and re-layouts: 5 us -> 7.19 us
    pallas_call x12, Pallas kernels: 35.1 us -> 32.9 us  [call(): pl.pallas_call(kernel, out_shape=[jax.ShapeDtypeStruct(shape, dtype) for...]
    all_to_all x1, blocking collectives: 19.8 us -> 18 us  [all_to_all(): return lax.all_to_all(x, axes, 0, 0, axis_index_groups=groups, tiled=True)]
  transfers between devices with their start and end apart: 28 -> 28, of which waited for: 13 -> 13; matrix products, arithmetic and copies ran while one was open for 0% -> 1% of each run, Pallas kernels for 16% -> 15%
where the time goes in v3:
time: 178 us; the launch traced here: 177 us
  waiting for transfers between devices  57.6 us (32%)
  starting transfers between devices  56.6 us (32%)
  Pallas kernels  32.9 us (18%)
  blocking collectives  18 us (10%)
  local copies, waits for them, and re-layouts  7.19 us (4%)
  other arithmetic  4.26 us (2%)
    ppermute x26, starting transfers between devices, hop(): lax.ppermute(x, 'blocks', [(i, (i + shift(i)) % size) for i in range(size)])  46.4 us
    ppermute x26, waiting for transfers between devices, hop(): lax.ppermute(x, 'blocks', [(i, (i + shift(i)) % size) for i in range(size)])  44.8 us
    pallas_call x12, Pallas kernels, call(): pl.pallas_call(kernel, out_shape=[jax.ShapeDtypeStruct(shape, dtype) for...  32.9 us
    all_to_all x1, blocking collectives, all_to_all(): return lax.all_to_all(x, axes, 0, 0, axis_index_groups=groups, tiled=True)  18 us
    all_to_all x2, waiting for transfers between devices, all_to_all(): return lax.all_to_all(x, axes, 0, 0, axis_index_groups=groups, tiled=True)  12.8 us
    all_to_all x2, starting transfers between devices, all_to_all(): return lax.all_to_all(x, axes, 0, 0, axis_index_groups=groups, tiled=True)  10.2 us
    unnamed x28, local copies, waits for them, and re-layouts  7.19 us
  transfers between devices with their start and end apart: 28, of which 13 were waited for; matrix products, arithmetic and copies ran while one was open for 1% of the time, Pallas kernels for 15%

profile of v3, /device:TPU:1, one launch (start us, length us, event | category | flops | bytes accessed | tf_op | source)
XLA Modules:
  0.0 177.4 jit_solution(8274339165500346719)
XLA Ops:
  3.1 8.7 %collective-permute-start.6 = (bf16[896,128]{1,0:T(8,128)(2,1)S(1)}, bf16[896,128]{1,0:T(8,128)(2,1)S(1)}, u32[]{:S(2)}, u32[]{:S(2)}) collective-permute-start(bf16[896,128]{1,0:T(8,128)(2,1)S(1)} %get-tuple-element.63.down.refs_0_), channel_id=1, source_target_pairs={{0,248},{4,252},{8,0},{12,4},{16,8},{20,12},{24,16},{28,20},{32,24... | collective-permute-start | bytes 688136 | tf_op jit(solution)/shard_map/ppermute | solution.py:348
  13.6 4.9 %collective-permute-start = (bf16[896,128]{1,0:T(8,128)(2,1)S(1)}, bf16[896,128]{1,0:T(8,128)(2,1)S(1)}, u32[]{:S(2)}, u32[]{:S(2)}) collective-permute-start(bf16[896,128]{1,0:T(8,128)(2,1)S(1)} %get-tuple-element.57.down.refs_0_), channel_id=1, source_target_pairs={{0,248},{4,252},{8,0},{12,4},{16,8},{20,12},{24,16},{28,20},{32,24... | collective-permute-start | bytes 688136 | tf_op jit(solution)/shard_map/ppermute | solution.py:348
  23.9 3.6 %collective-permute-done.1.u1.refs_3_ = bf16[896,128]{1,0:T(8,128)(2,1)S(1)} collective-permute-done((bf16[896,128]{1,0:T(8,128)(2,1)S(1)}, bf16[896,128]{1,0:T(8,128)(2,1)S(1)}, u32[]{:S(2)}, u32[]{:S(2)}) %collective-permute-start.1) | collective-permute-done | bytes 229408 | tf_op jit(solution)/shard_map/ppermute | solution.py:348
  28.1 2.5 %collective-permute-start.4 = (bf16[2688,128]{1,0:T(8,128)(2,1)S(1)}, bf16[2688,128]{1,0:T(8,128)(2,1)S(1)}, u32[]{:S(2)}, u32[]{:S(2)}) collective-permute-start(bf16[2688,128]{1,0:T(8,128)(2,1)S(1)} %get-tuple-element.61), channel_id=1, source_target_pairs={{0,4},{4,0},{8,12},{12,8},{16,20},{20,16},{24,28},{28,24},{32,36},... | collective-permute-start | bytes 2064392 | tf_op jit(solution)/shard_map/ppermute | solution.py:348
  30.6 2.4 %collective-permute-start.10 = (bf16[640,128]{1,0:T(8,128)(2,1)S(1)}, bf16[640,128]{1,0:T(8,128)(2,1)S(1)}, u32[]{:S(2)}, u32[]{:S(2)}) collective-permute-start(bf16[640,128]{1,0:T(8,128)(2,1)S(1)} %get-tuple-element.69), channel_id=1, source_target_pairs={{0,16},{4,20},{8,24},{12,28},{16,32},{20,36},{24,40},{28,44},{32,4... | collective-permute-start | bytes 491528 | tf_op jit(solution)/shard_map/ppermute | solution.py:348
  33.0 6.0 %collective-permute-done.9.refs_5_ = bf16[640,128]{1,0:T(8,128)(2,1)S(1)} collective-permute-done((bf16[640,128]{1,0:T(8,128)(2,1)S(1)}, bf16[640,128]{1,0:T(8,128)(2,1)S(1)}, u32[]{:S(2)}, u32[]{:S(2)}) %collective-permute-start.9) | collective-permute-done | bytes 163872 | tf_op jit(solution)/shard_map/ppermute | solution.py:348
  42.6 4.6 %collective-permute-done.8.refs_4_ = bf16[256,128]{1,0:T(8,128)(2,1)S(1)} collective-permute-done((bf16[256,128]{1,0:T(8,128)(2,1)S(1)}, bf16[256,128]{1,0:T(8,128)(2,1)S(1)}, u32[]{:S(2)}, u32[]{:S(2)}) %collective-permute-start.8) | collective-permute-done | bytes 65568 | tf_op jit(solution)/shard_map/ppermute | solution.py:348
  47.1 6.2 %collective-permute-start.2 = (bf16[640,128]{1,0:T(8,128)(2,1)S(1)}, bf16[640,128]{1,0:T(8,128)(2,1)S(1)}, u32[]{:S(2)}, u32[]{:S(2)}) collective-permute-start(bf16[640,128]{1,0:T(8,128)(2,1)S(1)} %get-tuple-element.59), channel_id=1, source_target_pairs={{0,240},{4,244},{8,248},{12,252},{16,0},{20,4},{24,8},{28,12},{32,... | collective-permute-start | bytes 491528 | tf_op jit(solution)/shard_map/ppermute | solution.py:348
  53.5 6.7 %shard_map.81 = (bf16[4,512,128]{2,1,0:T(8,128)(2,1)S(1)}, bf16[2048,128]{1,0:T(8,128)(2,1)S(1)}, f32[2048,128]{1,0:T(8,128)S(1)}, bf16[896,128]{1,0:T(8,128)(2,...) custom-call(s32[4,26]{1,0:T(4,128)S(1)} %bitcast.27, ...), custom_call_target="tpu_custom_call" | custom-call | tf_op jit(solution)/shard_map/pallas_call | solution.py:336
  60.8 4.9 %collective-permute-done.3.refs_6_ = bf16[640,128]{1,0:T(8,128)(2,1)S(1)} collective-permute-done((bf16[640,128]{1,0:T(8,128)(2,1)S(1)}, bf16[640,128]{1,0:T(8,128)(2,1)S(1)}, u32[]{:S(2)}, u32[]{:S(2)}) %collective-permute-start.3) | collective-permute-done | bytes 163872 | tf_op jit(solution)/shard_map/ppermute | solution.py:348
  65.7 2.8 %collective-permute-start.14 = (bf16[896,128]{1,0:T(8,128)(2,1)S(1)}, bf16[896,128]{1,0:T(8,128)(2,1)S(1)}, u32[]{:S(2)}, u32[]{:S(2)}) collective-permute-start(bf16[896,128]{1,0:T(8,128)(2,1)S(1)} %get-tuple-element.74.down.refs_0_), channel_id=1, source_target_pairs={{0,248},{4,252},{8,0},{12,4},{16,8},{20,12},{24,16},{28,20},{32,24... | collective-permute-start | bytes 688136 | tf_op jit(solution)/shard_map/ppermute | solution.py:348
  70.4 6.8 %shard_map.82 = (bf16[3,2,10,10,16,128]{5,4,3,2,1,0:T(8,128)(2,1)S(1)}, bf16[128,2048]{1,0:T(8,128)(2,1)S(1)}, bf16[128,2048]{1,0:T(8,128)(2,1)S(1)}) custom-call(s32[4,26]{1,0:T(4,128)S(1)} %bitcast.28, s32[1]{0:T(128)} %bitcast.1.dev, bf16[4,512,128]{2,1,0:T(8,128)(2,1)S(1)} %bitcast.20, bf16[896,128]{1,0:T(8,128)(2,1)S(1)} %get-tuple-element.57.down.refs_0_, ...), custom_call_target="tpu_custom_call" | custom-call | tf_op jit(solution)/shard_map/pallas_call | solution.py:336
  77.2 5.3 %shard_map.83 = (f32[3456,128]{1,0:T(8,128)S(1)}, f32[3456,128]{1,0:T(8,128)S(1)}) custom-call(s32[4,26]{1,0:T(4,128)S(1)} %bitcast.29, s32[1]{0:T(128)} %bitcast.1.dev, bf16[128,2048]{1,0:T(8,128)(2,1)S(1)} %get-tuple-element.86.hid_t, bf16[128,2048]{1,0:T(8,128)(2,1)S(1)} %get-tuple-element.87.delta_t, ...), custom_call_target="tpu_custom_call" | custom-call | tf_op jit(solution)/shard_map/pallas_call | solution.py:336
  84.7 2.8 %collective-permute-start.20 = (bf16[640,128]{1,0:T(8,128)(2,1)S(1)}, bf16[640,128]{1,0:T(8,128)(2,1)S(1)}, u32[]{:S(2)}, u32[]{:S(2)}) collective-permute-start(bf16[640,128]{1,0:T(8,128)(2,1)S(1)} %get-tuple-element.95), channel_id=1, source_target_pairs={{0,16},{4,20},{8,24},{12,28},{16,32},{20,36},{24,40},{28,44},{32,4... | collective-permute-start | bytes 491528 | tf_op jit(solution)/shard_map/ppermute | solution.py:348
  89.2 6.0 %collective-permute-done.19.refs_5_ = bf16[640,128]{1,0:T(8,128)(2,1)S(1)} collective-permute-done((bf16[640,128]{1,0:T(8,128)(2,1)S(1)}, bf16[640,128]{1,0:T(8,128)(2,1)S(1)}, u32[]{:S(2)}, u32[]{:S(2)}) %collective-permute-start.19) | collective-permute-done | bytes 163872 | tf_op jit(solution)/shard_map/ppermute | solution.py:348
  95.2 3.4 %collective-permute-done.20.refs_6_ = bf16[640,128]{1,0:T(8,128)(2,1)S(1)} collective-permute-done((bf16[640,128]{1,0:T(8,128)(2,1)S(1)}, bf16[640,128]{1,0:T(8,128)(2,1)S(1)}, u32[]{:S(2)}, u32[]{:S(2)}) %collective-permute-start.20) | collective-permute-done | bytes 163872 | tf_op jit(solution)/shard_map/ppermute | solution.py:348
  99.2 4.4 %all-to-all-start = ((bf16[16,216,128]{2,1,0:T(8,128)(2,1)}), bf16[16,216,128]{2,1,0:T(8,128)(2,1)S(1)}, u32[]{:S(2)}, u32[]{:S(2)}) async-start(bf16[16,216,128]{2,1,0:T(8,128)(2,1)} %bitcast.35), calls=%async_computation | async-start | bytes 1769472 | tf_op jit(solution)/shard_map/all_to_all | solution.py:418
  104.7 12.8 %all-to-all-done.parts = bf16[16,216,128]{2,1,0:T(8,128)(2,1)S(1)} async-done(((bf16[16,216,128]{2,1,0:T(8,128)(2,1)}), bf16[16,216,128]{2,1,0:T(8,128)(2,1)S(1)}, u32[]{:S(2)}, u32[]{:S(2)}) %all-to-all-start) | async-done | bytes 884768 | tf_op jit(solution)/shard_map/all_to_all | solution.py:418
  119.0 5.7 %all-to-all-start.1 = ((bf16[8,216,128]{2,1,0:T(8,128)(2,1)}), bf16[8,216,128]{2,1,0:T(8,128)(2,1)S(1)}, u32[]{:S(2)}, u32[]{:S(2)}) async-start(bf16[8,216,128]{2,1,0:T(8,128)(2,1)} %shard_map.85), calls=%async_computation.1 | async-start | bytes 884736 | tf_op jit(solution)/shard_map/all_to_all | solution.py:418
  124.7 8.6 %collective-permute-start.24 = (bf16[256,128]{1,0:T(8,128)(2,1)}, bf16[256,128]{1,0:T(8,128)(2,1)S(1)}, u32[]{:S(2)}, u32[]{:S(2)}) collective-permute-start(bf16[256,128]{1,0:T(8,128)(2,1)} %copy-done.13), channel_id=1, source_target_pairs={{0,228},{4,32},{8,236},{12,40},{16,244},{20,48},{24,252},{28,56},{... | collective-permute-start | bytes 196616 | tf_op jit(solution)/shard_map/ppermute | solution.py:348
  133.4 10.2 %collective-permute-done.24.refs_4_ = bf16[256,128]{1,0:T(8,128)(2,1)S(1)} collective-permute-done((bf16[256,128]{1,0:T(8,128)(2,1)}, bf16[256,128]{1,0:T(8,128)(2,1)S(1)}, u32[]{:S(2)}, u32[]{:S(2)}) %collective-permute-start.24) | collective-permute-done | bytes 65568 | tf_op jit(solution)/shard_map/ppermute | solution.py:348
  145.5 7.7 %shard_map.87 = bf16[4,512,128]{2,1,0:T(8,128)(2,1)} custom-call(s32[4,26]{1,0:T(4,128)S(1)} %bitcast.32, s32[1]{0:T(128)} %bitcast.1.dev, bf16[4,512,128]{2,1,0:T(8,128)(2,1)S(1)} %copy-done.8, bf16[896,128]{1,0:T(8,128)(2,1)S(1)} %get-tuple-element.74.down.refs_0_, bf16[896,128]{1,0:T(8,128)(2,1)S(1)} %get-tuple-element.75.up.refs_1_, ...), custom_call_target="tpu_custom_call" | custom-call | tf_op jit(solution)/shard_map/pallas_call | solution.py:336
  153.8 18.0 %all_to_all.15 = bf16[16,216,128]{2,1,0:T(8,128)(2,1)S(1)} all-to-all(bf16[16,216,128]{2,1,0:T(8,128)(2,1)S(1)} %shard_map.86), channel_id=1, replica_groups={{0,1,2,3,64,65,66,67,128,129,130,131,192,193,194,195},{4,5,6,7,68,69,70..., dimensions={0} | all-to-all | bytes 1769472 | tf_op jit(solution)/shard_map/all_to_all | solution.py:418
  171.9 2.4 %collective-permute-done.25 = bf16[3456,128]{1,0:T(8,128)(2,1)S(1)} collective-permute-done((bf16[3456,128]{1,0:T(8,128)(2,1)S(1)}, bf16[3456,128]{1,0:T(8,128)(2,1)S(1)}, u32[]{:S(2)}, u32[]{:S(2)}) %collective-permute-start.25) | collective-permute-done | bytes 884768 | tf_op jit(solution)/shard_map/ppermute | solution.py:348
  (77 shorter events, 29.3 us)
Async XLA Ops:
  3.1 17.4 %collective-permute-start.6 = (bf16[896,128]{1,0:T(8,128)(2,1)S(1)}, bf16[896,128]{1,0:T(8,128)(2,1)S(1)}, u32[]{:S(2)}, u32[]{:S(2)}) collective-permute-start(bf16[896,128]{1,0:T(8,128)(2,1)S(1)} %get-tuple-element.63.down.refs_0_), channel_id=1, source_target_pairs={{0,248},{4,252},{8,0},{12,4},{16,8},{20,12},{24,16},{28,20},{32,24... | collective-permute-start | bytes 688136 | tf_op jit(solution)/shard_map/ppermute | solution.py:348
  11.8 9.5 %collective-permute-start.7 = (bf16[896,128]{1,0:T(8,128)(2,1)S(1)}, bf16[896,128]{1,0:T(8,128)(2,1)S(1)}, u32[]{:S(2)}, u32[]{:S(2)}) collective-permute-start(bf16[896,128]{1,0:T(8,128)(2,1)S(1)} %get-tuple-element.64.up.refs_1_), channel_id=1, source_target_pairs={{0,8},{4,12},{8,16},{12,20},{16,24},{20,28},{24,32},{28,36},{32,40... | collective-permute-start | bytes 688136 | tf_op jit(solution)/shard_map/ppermute | solution.py:348
  13.6 10.3 %collective-permute-start = (bf16[896,128]{1,0:T(8,128)(2,1)S(1)}, bf16[896,128]{1,0:T(8,128)(2,1)S(1)}, u32[]{:S(2)}, u32[]{:S(2)}) collective-permute-start(bf16[896,128]{1,0:T(8,128)(2,1)S(1)} %get-tuple-element.57.down.refs_0_), channel_id=1, source_target_pairs={{0,248},{4,252},{8,0},{12,4},{16,8},{20,12},{24,16},{28,20},{32,24... | collective-permute-start | bytes 688136 | tf_op jit(solution)/shard_map/ppermute | solution.py:348
  18.5 9.0 %collective-permute-start.1 = (bf16[896,128]{1,0:T(8,128)(2,1)S(1)}, bf16[896,128]{1,0:T(8,128)(2,1)S(1)}, u32[]{:S(2)}, u32[]{:S(2)}) collective-permute-start(bf16[896,128]{1,0:T(8,128)(2,1)S(1)} %get-tuple-element.58.up.refs_1_), channel_id=1, source_target_pairs={{0,8},{4,12},{8,16},{12,20},{16,24},{20,28},{24,32},{28,36},{32,40... | collective-permute-start | bytes 688136 | tf_op jit(solution)/shard_map/ppermute | solution.py:348
  22.0 31.4 %collective-permute-start.11 = (bf16[2688,128]{1,0:T(8,128)(2,1)S(1)}, bf16[2688,128]{1,0:T(8,128)(2,1)S(1)}, u32[]{:S(2)}, u32[]{:S(2)}) collective-permute-start(bf16[2688,128]{1,0:T(8,128)(2,1)S(1)} %get-tuple-element.70), channel_id=1, source_target_pairs={{0,4},{4,0},{8,12},{12,8},{16,20},{20,16},{24,28},{28,24},{32,36},... | collective-permute-start | bytes 2064392 | tf_op jit(solution)/shard_map/ppermute | solution.py:348
  28.1 37.6 %collective-permute-start.4 = (bf16[2688,128]{1,0:T(8,128)(2,1)S(1)}, bf16[2688,128]{1,0:T(8,128)(2,1)S(1)}, u32[]{:S(2)}, u32[]{:S(2)}) collective-permute-start(bf16[2688,128]{1,0:T(8,128)(2,1)S(1)} %get-tuple-element.61), channel_id=1, source_target_pairs={{0,4},{4,0},{8,12},{12,8},{16,20},{20,16},{24,28},{28,24},{32,36},... | collective-permute-start | bytes 2064392 | tf_op jit(solution)/shard_map/ppermute | solution.py:348
  30.6 8.3 %collective-permute-start.9 = (bf16[640,128]{1,0:T(8,128)(2,1)S(1)}, bf16[640,128]{1,0:T(8,128)(2,1)S(1)}, u32[]{:S(2)}, u32[]{:S(2)}) collective-permute-start(bf16[640,128]{1,0:T(8,128)(2,1)S(1)} %get-tuple-element.68), channel_id=1, source_target_pairs={{0,240},{4,244},{8,248},{12,252},{16,0},{20,4},{24,8},{28,12},{32,... | collective-permute-start | bytes 491528 | tf_op jit(solution)/shard_map/ppermute | solution.py:348
  30.6 10.9 %collective-permute-start.10 = (bf16[640,128]{1,0:T(8,128)(2,1)S(1)}, bf16[640,128]{1,0:T(8,128)(2,1)S(1)}, u32[]{:S(2)}, u32[]{:S(2)}) collective-permute-start(bf16[640,128]{1,0:T(8,128)(2,1)S(1)} %get-tuple-element.69), channel_id=1, source_target_pairs={{0,16},{4,20},{8,24},{12,28},{16,32},{20,36},{24,40},{28,44},{32,4... | collective-permute-start | bytes 491528 | tf_op jit(solution)/shard_map/ppermute | solution.py:348
  38.9 14.4 %collective-permute-start.12 = (bf16[640,128]{1,0:T(8,128)(2,1)S(1)}, bf16[640,128]{1,0:T(8,128)(2,1)S(1)}, u32[]{:S(2)}, u32[]{:S(2)}) collective-permute-start(bf16[640,128]{1,0:T(8,128)(2,1)S(1)} %collective-permute-done.9.refs_5_), channel_id=1, source_target_pairs={{0,4},{4,0},{8,12},{12,8},{16,20},{20,16},{24,28},{28,24},{32,36},... | collective-permute-start | bytes 491528 | tf_op jit(solution)/shard_map/ppermute | solution.py:348
  39.9 7.2 %collective-permute-start.8 = (bf16[256,128]{1,0:T(8,128)(2,1)S(1)}, bf16[256,128]{1,0:T(8,128)(2,1)S(1)}, u32[]{:S(2)}, u32[]{:S(2)}) collective-permute-start(bf16[256,128]{1,0:T(8,128)(2,1)S(1)} %get-tuple-element.67), channel_id=1, source_target_pairs={{0,236},{4,24},{8,244},{12,32},{16,252},{20,40},{24,4},{28,48},{32... | collective-permute-start | bytes 196616 | tf_op jit(solution)/shard_map/ppermute | solution.py:348
  41.5 11.8 %collective-permute-start.13 = (bf16[640,128]{1,0:T(8,128)(2,1)S(1)}, bf16[640,128]{1,0:T(8,128)(2,1)S(1)}, u32[]{:S(2)}, u32[]{:S(2)}) collective-permute-start(bf16[640,128]{1,0:T(8,128)(2,1)S(1)} %collective-permute-done.10.refs_6_), channel_id=1, source_target_pairs={{0,4},{4,0},{8,12},{12,8},{16,20},{20,16},{24,28},{28,24},{32,36},... | collective-permute-start | bytes 491528 | tf_op jit(solution)/shard_map/ppermute | solution.py:348
  47.1 13.7 %collective-permute-start.2 = (bf16[640,128]{1,0:T(8,128)(2,1)S(1)}, bf16[640,128]{1,0:T(8,128)(2,1)S(1)}, u32[]{:S(2)}, u32[]{:S(2)}) collective-permute-start(bf16[640,128]{1,0:T(8,128)(2,1)S(1)} %get-tuple-element.59), channel_id=1, source_target_pairs={{0,240},{4,244},{8,248},{12,252},{16,0},{20,4},{24,8},{28,12},{32,... | collective-permute-start | bytes 491528 | tf_op jit(solution)/shard_map/ppermute | solution.py:348
  53.3 12.4 %collective-permute-start.3 = (bf16[640,128]{1,0:T(8,128)(2,1)S(1)}, bf16[640,128]{1,0:T(8,128)(2,1)S(1)}, u32[]{:S(2)}, u32[]{:S(2)}) collective-permute-start(bf16[640,128]{1,0:T(8,128)(2,1)S(1)} %get-tuple-element.60), channel_id=1, source_target_pairs={{0,16},{4,20},{8,24},{12,28},{16,32},{20,36},{24,40},{28,44},{32,4... | collective-permute-start | bytes 491528 | tf_op jit(solution)/shard_map/ppermute | solution.py:348
  53.3 7.5 %collective-permute-start.5 = (bf16[256,128]{1,0:T(8,128)(2,1)S(1)}, bf16[256,128]{1,0:T(8,128)(2,1)S(1)}, u32[]{:S(2)}, u32[]{:S(2)}) collective-permute-start(bf16[256,128]{1,0:T(8,128)(2,1)S(1)} %get-tuple-element.62), channel_id=1, source_target_pairs={{0,236},{4,24},{8,244},{12,32},{16,252},{20,40},{24,4},{28,48},{32... | collective-permute-start | bytes 196616 | tf_op jit(solution)/shard_map/ppermute | solution.py:348
  65.7 11.5 %collective-permute-start.14 = (bf16[896,128]{1,0:T(8,128)(2,1)S(1)}, bf16[896,128]{1,0:T(8,128)(2,1)S(1)}, u32[]{:S(2)}, u32[]{:S(2)}) collective-permute-start(bf16[896,128]{1,0:T(8,128)(2,1)S(1)} %get-tuple-element.74.down.refs_0_), channel_id=1, source_target_pairs={{0,248},{4,252},{8,0},{12,4},{16,8},{20,12},{24,16},{28,20},{32,24... | collective-permute-start | bytes 688136 | tf_op jit(solution)/shard_map/ppermute | solution.py:348
  68.6 8.7 %collective-permute-start.15 = (bf16[896,128]{1,0:T(8,128)(2,1)S(1)}, bf16[896,128]{1,0:T(8,128)(2,1)S(1)}, u32[]{:S(2)}, u32[]{:S(2)}) collective-permute-start(bf16[896,128]{1,0:T(8,128)(2,1)S(1)} %get-tuple-element.75.up.refs_1_), channel_id=1, source_target_pairs={{0,8},{4,12},{8,16},{12,20},{16,24},{20,28},{24,32},{28,36},{32,40... | collective-permute-start | bytes 688136 | tf_op jit(solution)/shard_map/ppermute | solution.py:348
  83.5 11.7 %collective-permute-start.19 = (bf16[640,128]{1,0:T(8,128)(2,1)S(1)}, bf16[640,128]{1,0:T(8,128)(2,1)S(1)}, u32[]{:S(2)}, u32[]{:S(2)}) collective-permute-start(bf16[640,128]{1,0:T(8,128)(2,1)S(1)} %get-tuple-element.94), channel_id=1, source_target_pairs={{0,240},{4,244},{8,248},{12,252},{16,0},{20,4},{24,8},{28,12},{32,... | collective-permute-start | bytes 491528 | tf_op jit(solution)/shard_map/ppermute | solution.py:348
  84.7 13.9 %collective-permute-start.20 = (bf16[640,128]{1,0:T(8,128)(2,1)S(1)}, bf16[640,128]{1,0:T(8,128)(2,1)S(1)}, u32[]{:S(2)}, u32[]{:S(2)}) collective-permute-start(bf16[640,128]{1,0:T(8,128)(2,1)S(1)} %get-tuple-element.95), channel_id=1, source_target_pairs={{0,16},{4,20},{8,24},{12,28},{16,32},{20,36},{24,40},{28,44},{32,4... | collective-permute-start | bytes 491528 | tf_op jit(solution)/shard_map/ppermute | solution.py:348
  87.4 11.1 %collective-permute-start.21 = (bf16[2688,128]{1,0:T(8,128)(2,1)S(1)}, bf16[2688,128]{1,0:T(8,128)(2,1)S(1)}, u32[]{:S(2)}, u32[]{:S(2)}) collective-permute-start(bf16[2688,128]{1,0:T(8,128)(2,1)S(1)} %get-tuple-element.96), channel_id=1, source_target_pairs={{0,4},{4,0},{8,12},{12,8},{16,20},{20,16},{24,28},{28,24},{32,36},... | collective-permute-start | bytes 2064392 | tf_op jit(solution)/shard_map/ppermute | solution.py:348
  99.2 18.3 %all-to-all-start = ((bf16[16,216,128]{2,1,0:T(8,128)(2,1)}), bf16[16,216,128]{2,1,0:T(8,128)(2,1)S(1)}, u32[]{:S(2)}, u32[]{:S(2)}) async-start(bf16[16,216,128]{2,1,0:T(8,128)(2,1)} %bitcast.35), calls=%async_computation | async-start | bytes 1769472 | tf_op jit(solution)/shard_map/all_to_all | solution.py:418
  103.7 15.3 %collective-permute-start.22 = (bf16[640,128]{1,0:T(8,128)(2,1)S(1)}, bf16[640,128]{1,0:T(8,128)(2,1)}, u32[]{:S(2)}, u32[]{:S(2)}) collective-permute-start(bf16[640,128]{1,0:T(8,128)(2,1)S(1)} %collective-permute-done.19.refs_5_), channel_id=1, source_target_pairs={{0,4},{4,0},{8,12},{12,8},{16,20},{20,16},{24,28},{28,24},{32,36},... | collective-permute-start | bytes 491528 | tf_op jit(solution)/shard_map/ppermute | solution.py:348
  104.6 14.4 %collective-permute-start.23 = (bf16[640,128]{1,0:T(8,128)(2,1)}, bf16[640,128]{1,0:T(8,128)(2,1)}, u32[]{:S(2)}, u32[]{:S(2)}) collective-permute-start(bf16[640,128]{1,0:T(8,128)(2,1)} %copy-done.11), channel_id=1, source_target_pairs={{0,4},{4,0},{8,12},{12,8},{16,20},{20,16},{24,28},{28,24},{32,36},... | collective-permute-start | bytes 491528 | tf_op jit(solution)/shard_map/ppermute | solution.py:348
  119.0 34.2 %all-to-all-start.1 = ((bf16[8,216,128]{2,1,0:T(8,128)(2,1)}), bf16[8,216,128]{2,1,0:T(8,128)(2,1)S(1)}, u32[]{:S(2)}, u32[]{:S(2)}) async-start(bf16[8,216,128]{2,1,0:T(8,128)(2,1)} %shard_map.85), calls=%async_computation.1 | async-start | bytes 884736 | tf_op jit(solution)/shard_map/all_to_all | solution.py:418
  124.7 18.8 %collective-permute-start.24 = (bf16[256,128]{1,0:T(8,128)(2,1)}, bf16[256,128]{1,0:T(8,128)(2,1)S(1)}, u32[]{:S(2)}, u32[]{:S(2)}) collective-permute-start(bf16[256,128]{1,0:T(8,128)(2,1)} %copy-done.13), channel_id=1, source_target_pairs={{0,228},{4,32},{8,236},{12,40},{16,244},{20,48},{24,252},{28,56},{... | collective-permute-start | bytes 196616 | tf_op jit(solution)/shard_map/ppermute | solution.py:348
  (18 other events, 191.6 us)
